TPU v7x, 256 devices: a whole 4x4x8 slice. The times are simulated.
256 devices in a mesh: front: 16 (over z, core), row: 4 (over y), col: 4 (over x).
Axes of the slice: x: 4, y: 4, z: 8, core: 2. Of those that a mesh axis runs over, the one named last changes fastest.
Arguments:
- ancestor: bfloat16 [32768, 256], P('front'), may hold values from -6 to 6
- send_rows: int32 [16, 16, 4, 256], P('front', None, 'col'), may hold values from 0 to 2047, as said below
- send_count: int32 [16, 16, 4], P('front', None, 'col'), may hold values from 1 to 256, as said below
- border_coeff: bfloat16 [16, 4096, 16384], P('front', 'row', 'col'), may hold values from -0.0625 to 0.0625
- right_side: bfloat16 [16, 4096, 256], P('front', 'row'), may hold values from -6 to 6
- pivot_inverse: bfloat16 [16, 4096, 4096], P('front', 'row', 'col'), may hold values from -0.09375 to 0.09375
Outputs:
- solution: float32 [16, 256, 4096], P('front', 'row', 'col')
Inputs may be any that keep to these rules, and one draw needn't show every extreme that they name: `send_rows`: row lists index the holder's own ancestor rows; entries past a slot's count are padding. `send_count`: loads differ from front to front; in every draw one front receives 256 rows from every holder in every column block.
All inputs are finite; a program needn't handle non-finite values.
Results may differ from a plain program's by a relative error of at most 0.015.
Values may be sent and summed in bfloat16 or wider, within the bound.
No kernel may reach another device: no remote copies, remote signals or barrier semaphores. Data moves between devices by JAX's collectives and lax.ppermute only.
A program may use at most 64 MiB of HBM per device.

v0:
```python
import functools

import jax
import jax.numpy as jnp
from jax import lax
from jax.experimental import pallas as pl
from jax.experimental.pallas import tpu as pltpu
from jax.sharding import PartitionSpec as P


def shifted(shard, axis, step):
    peers = lax.axis_size(axis)
    return lax.ppermute(shard, axis, [(i, (i + step) % peers) for i in range(peers)])


def even_swap(shard, axis):
    peers = lax.axis_size(axis)
    return lax.ppermute(shard, axis, [(i, i ^ 1) for i in range(peers)])


def odd_swap(shard, axis):
    peers = lax.axis_size(axis)
    return lax.ppermute(shard, axis, [(i, (i + (1 if i % 2 else -1)) % peers) for i in range(peers)])


FAR = (4, 3, -3)
MID = (2, -2)
NEAR = (1, -1, 0)
CHIPS = 8


def along_chips(shard, step):
    peers = lax.axis_size("front")
    return lax.ppermute(shard, "front", [(i, (i + 2 * step) % peers) for i in range(peers)])


def place():
    front = lax.axis_index("front")
    return lax.shift_right_logical(front, 1), lax.bitwise_and(front, 1)


def picked_rows(ancestor, index):
    row = lax.broadcasted_iota(jnp.int32, (ancestor.shape[0], index.shape[1]), 0)
    chosen = (row == index).astype(jnp.bfloat16)
    return lax.dot_general(
        chosen, ancestor, (((0,), (0,)), ((), ())), preferred_element_type=jnp.float32
    ).astype(jnp.bfloat16)


def pick_shares_kernel(
    counts_hbm, lists_hbm, ancestor_hbm, kept_ref, sent_ref, live_ref, held_ref, counts_ref, sems
):
    copies = [
        pltpu.make_async_copy(source, target, sems.at[i])
        for i, (source, target) in enumerate(
            ((counts_hbm, counts_ref), (lists_hbm.at[0], live_ref), (ancestor_hbm, held_ref))
        )
    ]
    for copy in copies:
        copy.start()
    for copy in copies[:2]:
        copy.wait()
    slot_rows = live_ref.shape[-1]
    share = slot_rows // lax.axis_size("row")
    first = lax.axis_index("row") * share
    chip, core = place()
    lane = lax.broadcasted_iota(jnp.int32, (1, 2 * share), 1)
    slot = lax.broadcasted_iota(jnp.int32, (1, slot_rows), 1)
    for d in range(live_ref.shape[0]):
        live_ref[d] = jnp.where(slot < counts_ref[d], live_ref[d], -1)

    def rolled(d, start):
        row = jnp.broadcast_to(live_ref[d], (8, slot_rows))
        return pltpu.roll(row, lax.rem(slot_rows - first + start, slot_rows), 1)[:1, : 2 * share]

    chosen = []
    for step in FAR:
        target = 2 * lax.rem(chip + step + CHIPS, CHIPS)
        kept, sent = rolled(target + core, 0), rolled(target + 1 - core, share)
        chosen.append(jnp.where(lane < share, kept, sent))
    copies[2].wait()
    for i, index in enumerate(chosen):
        rows = picked_rows(held_ref[...], index)
        kept_ref[i] = rows[:share]
        sent_ref[i] = rows[share:]


def pick_slots_kernel(steps, live_ref, held_ref, kept_ref, sent_ref):
    chip, core = place()
    ancestor = held_ref[...]
    for i, step in enumerate(steps):
        target = 2 * lax.rem(chip + step + CHIPS, CHIPS)
        for d, ref in ((target + 1 - core, sent_ref), (target + core, kept_ref)):
            ref[i] = picked_rows(ancestor, live_ref[d])


def pick_shares(counts, lists, ancestor):
    share = lists.shape[-1] // lax.axis_size("row")
    vmem = pl.BlockSpec(memory_space=pltpu.VMEM)
    shape = jax.ShapeDtypeStruct((len(FAR), share, ancestor.shape[1]), ancestor.dtype)
    return pl.pallas_call(
        pick_shares_kernel,
        out_shape=(
            shape,
            shape,
            jax.ShapeDtypeStruct(lists.shape[1:], lists.dtype),
            jax.ShapeDtypeStruct(ancestor.shape, ancestor.dtype),
        ),
        in_specs=[pl.BlockSpec(memory_space=pltpu.HBM)] * 3,
        out_specs=(vmem,) * 4,
        scratch_shapes=[
            pltpu.SMEM(counts.shape, counts.dtype),
            pltpu.SemaphoreType.DMA((3,)),
        ],
        compiler_params=pltpu.CompilerParams(vmem_limit_bytes=24 << 20),
    )(*(pltpu.with_memory_space_constraint(x, pltpu.HBM) for x in (counts, lists, ancestor)))


def pick_slots(steps, lists, ancestor):
    vmem = pl.BlockSpec(memory_space=pltpu.VMEM)
    rows = lists.shape[-1]
    shape = jax.ShapeDtypeStruct((len(steps), rows, ancestor.shape[1]), ancestor.dtype)
    return pl.pallas_call(
        functools.partial(pick_slots_kernel, steps),
        out_shape=(shape, shape),
        in_specs=[vmem, vmem],
        out_specs=(vmem, vmem),
        compiler_params=pltpu.CompilerParams(vmem_limit_bytes=24 << 20),
        cost_estimate=pl.CostEstimate(
            flops=4 * len(steps) * rows * ancestor.size,
            bytes_accessed=2 * ancestor.size,
            transcendentals=0,
        ),
    )(lists, ancestor)


def columns(coeff_ref, chip, top, height):
    width = coeff_ref.shape[1] // CHIPS
    return coeff_ref[top : top + height, pl.ds(pl.multiple_of(chip * width, width), width)]


def near_kernel(coeff_ref, kept_ref, came_ref, *refs):
    *part_refs, sum_ref, rows_ref = refs
    chip, core = place()
    slot_rows = kept_ref.shape[0]
    kept, came = kept_ref[...], came_ref[...]
    rows_ref[0, :slot_rows] = jnp.where(core == 0, kept, came)
    rows_ref[0, slot_rows:] = jnp.where(core == 0, came, kept)
    pivots = coeff_ref.shape[0]
    sum_ref[...] = jnp.dot(
        columns(coeff_ref, chip, 0, pivots), rows_ref[0], preferred_element_type=jnp.float32
    )
    for i, (step, part_ref) in enumerate(zip(MID + NEAR[:2], part_refs, strict=True), 1):
        for holder in range(2):
            rows_ref[i, holder * slot_rows : (holder + 1) * slot_rows] = part_ref[
                lax.bitwise_xor(core, holder)
            ]
        sum_ref[...] += jnp.dot(
            columns(coeff_ref, lax.rem(chip - step + CHIPS, CHIPS), 0, pivots),
            rows_ref[i],
            preferred_element_type=jnp.float32,
        )


def far_kernel(
    part, coeff_ref, sum_ref, own_ref, across_ref, before_ref, after_ref, out_ref, rows_ref
):
    chip, core = place()
    me = lax.axis_index("row")
    peers = lax.axis_size("row")
    share = own_ref.shape[2]
    half = out_ref.shape[0]
    total = sum_ref[part * half : (part + 1) * half]
    for i, step in enumerate(FAR):
        for block in range(peers):
            back = lax.rem(block - me + peers, peers)
            for holder in range(2):
                piece = before_ref[i, lax.bitwise_xor(core, holder)]
                for away, part_ref in ((2, across_ref), (1, after_ref), (0, own_ref)):
                    piece = jnp.where(
                        back == away, part_ref[i, lax.bitwise_xor(core, holder)], piece
                    )
                start = (holder * peers + block) * share
                rows_ref[i, start : start + share, :] = piece
        total = total + jnp.dot(
            columns(coeff_ref, lax.rem(chip - step + CHIPS, CHIPS), part * half, half),
            rows_ref[i],
            preferred_element_type=jnp.float32,
        )
    out_ref[...] = total.astype(out_ref.dtype)


def products(coeff, kept, came, mid, near, shares):
    vmem = pl.BlockSpec(memory_space=pltpu.VMEM)
    pivots, sources = coeff.shape[0], kept.shape[-1]
    depth = coeff.shape[1] // CHIPS

    def cost(blocks):
        return pl.CostEstimate(
            flops=int(2 * blocks) * depth * pivots * sources,
            bytes_accessed=int(2 * blocks) * depth * (pivots + sources),
            transcendentals=0,
        )

    total = pl.pallas_call(
        near_kernel,
        out_shape=jax.ShapeDtypeStruct((pivots, sources), jnp.float32),
        in_specs=[vmem] * 7,
        out_specs=vmem,
        scratch_shapes=[pltpu.VMEM((len(MID + NEAR), depth, sources), coeff.dtype)],
        compiler_params=pltpu.CompilerParams(vmem_limit_bytes=24 << 20),
        cost_estimate=cost(5),
    )(coeff, kept, came, *mid, *near)
    half = jax.ShapeDtypeStruct((pivots // 2, sources), coeff.dtype)
    return [
        pl.pallas_call(
            functools.partial(far_kernel, part),
            out_shape=half,
            in_specs=[vmem] * 6,
            out_specs=vmem,
            scratch_shapes=[pltpu.VMEM((len(FAR), depth, sources), coeff.dtype)],
            compiler_params=pltpu.CompilerParams(vmem_limit_bytes=24 << 20),
            cost_estimate=cost(len(FAR) / 2),
        )(coeff, total, *shares)
        for part in range(2)
    ]


def added(a, b):
    return (a.astype(jnp.float32) + b.astype(jnp.float32)).astype(jnp.bfloat16)


def per_device(ancestor, send_rows, send_count, border_coeff, right_side, pivot_inverse):
    kept, sent, live, held = pick_shares(send_count.reshape(-1), send_rows, ancestor)
    came = even_swap(sent, "front")
    far = jnp.stack([kept, came], 1)
    kept, sent = pick_slots(NEAR, live, held)
    came = even_swap(sent, "front")
    near = jnp.stack([kept, came], 1)
    kept, sent = pick_slots(MID, live, held)
    came = even_swap(sent, "front")
    mid = jnp.stack([kept, came], 1)
    sent = []
    for part, steps in ((near, NEAR[:2]), (far, FAR), (mid, MID)):
        for i, step in enumerate(steps):
            sent.append(along_chips(part[i], step))
    near_parts, shares, mid_parts = sent[:2], jnp.stack(sent[2:5]), sent[5:]
    shares = [shares]
    for step in (2, 1, -1):
        shares.append(shifted(shares[0], "row", step))
    coeff = pltpu.with_memory_space_constraint(border_coeff[0], pltpu.VMEM)
    rhs = right_side[0]
    inverse = pivot_inverse[0]
    half = coeff.shape[0] // 2
    halves = products(coeff, near[2, 0], near[2, 1], mid_parts, near_parts, shares)
    parts = []
    for i, (one, two) in enumerate(((even_swap, odd_swap), (odd_swap, even_swap))):
        rows = slice(i * half, (i + 1) * half)
        pair = added(halves[i], one(halves[i], "col"))
        other = two(pair, "col")
        total = pair.astype(jnp.float32) + other.astype(jnp.float32)
        parts.append((rhs[rows].astype(jnp.float32) - total).astype(jnp.bfloat16))
    residual = jnp.concatenate(parts, 0)
    term = lax.dot_general(
        residual, inverse, (((0,), (0,)), ((), ())), preferred_element_type=jnp.float32
    ).astype(jnp.bfloat16)
    peers = lax.axis_size("row")
    tiles = term.reshape(peers, term.shape[0] // peers, term.shape[1])
    tiles = lax.all_to_all(tiles, "row", 0, 0, tiled=True)
    return jnp.sum(tiles.astype(jnp.float32), axis=0)[None]


def solution(mesh):
    return sharded(per_device, mesh)


def sharded(body, mesh):
    return jax.shard_map(
        body,
        mesh=mesh,
        in_specs=(
            P("front", None),
            P("front", None, "col", None),
            P("front", None, "col"),
            P("front", "row", "col"),
            P("front", "row", None),
            P("front", "row", "col"),
        ),
        out_specs=P("front", "row", "col"),
        check_vma=False,
    )
```

profile of v0, /device:TPU:32, one launch (start us, length us, event | category | flops | bytes accessed | tf_op | source)
XLA Modules:
  0.0 81.3 jit_solution(88669672081831714)
XLA Ops:
  0.0 2.0 %shard_map.64 = (bf16[3,64,256]{2,1,0:T(8,128)(2,1)S(1)}, bf16[3,64,256]{2,1,0:T(8,128)(2,1)S(1)}, s32[16,1,256]{2,1,0:T(1,128)S(1)}, bf16[2048,256]{1,0:T(8,128)(2,1)S(1)}) custom-call(s32[16]{0:T(128)} %bitcast.55, s32[1,16,1,256]{3,2,1,0:T(1,128)} %lists_hbm.1, bf16[2048,256]{1,0:T(8,128)(2,1)} %ancestor_hbm.1), custom_call_target="tpu_custom_call" | custom-call | tf_op jit(solution)/shard_map/pallas_call | solution.py:101
  2.1 1.3 %shard_map.66 = (bf16[2,256,256]{2,1,0:T(8,128)(2,1)S(1)}, bf16[2,256,256]{2,1,0:T(8,128)(2,1)S(1)}) custom-call(s32[16,1,256]{2,1,0:T(1,128)S(1)} %get-tuple-element.13.live_ref, bf16[2048,256]{1,0:T(8,128)(2,1)S(1)} %get-tuple-element.14.held_ref), custom_call_target="tpu_custom_call" | custom-call | flops 1073741824 | bytes 1048576 | tf_op jit(solution)/shard_map/pallas_call | solution.py:123
  3.4 0.1 collective-permute-start.1
  3.5 0.0 copy-start.1
  3.5 1.9 %shard_map.65 = (bf16[3,256,256]{2,1,0:T(8,128)(2,1)S(1)}, bf16[3,256,256]{2,1,0:T(8,128)(2,1)S(1)}) custom-call(s32[16,1,256]{2,1,0:T(1,128)S(1)} %get-tuple-element.13.live_ref, bf16[2048,256]{1,0:T(8,128)(2,1)S(1)} %get-tuple-element.14.held_ref), custom_call_target="tpu_custom_call" | custom-call | flops 1610612736 | bytes 1048576 | tf_op jit(solution)/shard_map/pallas_call | solution.py:123
  5.3 0.6 collective-permute-start
  5.9 0.1 collective-permute-start.6
  6.0 0.0 collective-permute-done.1
  6.1 3.3 %collective-permute-start.2 = (bf16[2,256,256]{2,1,0:T(8,128)(2,1)S(1)}, bf16[2,256,256]{2,1,0:T(8,128)(2,1)S(1)}, u32[]{:S(2)}, u32[]{:S(2)}) collective-permute-start(bf16[2,256,256]{2,1,0:T(8,128)(2,1)S(1)} %get-tuple-element.26), channel_id=1, source_target_pairs={{0,64},{16,80},{32,96},{48,112},{64,128},{80,144},{96,160},{112,17... | collective-permute-start | bytes 786440 | tf_op jit(solution)/shard_map/ppermute | solution.py:34
  9.4 2.2 %collective-permute-start.3 = (bf16[2,256,256]{2,1,0:T(8,128)(2,1)S(1)}, bf16[2,256,256]{2,1,0:T(8,128)(2,1)S(1)}, u32[]{:S(2)}, u32[]{:S(2)}) collective-permute-start(bf16[2,256,256]{2,1,0:T(8,128)(2,1)S(1)} %get-tuple-element.25), channel_id=1, source_target_pairs={{0,192},{16,208},{32,224},{48,240},{64,0},{80,16},{96,32},{112,48}... | collective-permute-start | bytes 786440 | tf_op jit(solution)/shard_map/ppermute | solution.py:34
  11.7 0.0 collective-permute-done.6
  11.7 3.3 %collective-permute-start.9 = (bf16[2,64,256]{2,1,0:T(8,128)(2,1)S(1)}, bf16[2,64,256]{2,1,0:T(8,128)(2,1)S(1)}, u32[]{:S(2)}, u32[]{:S(2)}) collective-permute-start(bf16[2,64,256]{2,1,0:T(8,128)(2,1)S(1)} %get-tuple-element.28), channel_id=1, source_target_pairs={{0,160},{16,176},{32,192},{48,208},{64,224},{80,240},{96,0},{112,1... | collective-permute-start | bytes 196616 | tf_op jit(solution)/shard_map/ppermute | solution.py:34
  15.1 1.8 %collective-permute-start.8 = (bf16[2,64,256]{2,1,0:T(8,128)(2,1)S(1)}, bf16[2,64,256]{2,1,0:T(8,128)(2,1)S(1)}, u32[]{:S(2)}, u32[]{:S(2)}) collective-permute-start(bf16[2,64,256]{2,1,0:T(8,128)(2,1)S(1)} %get-tuple-element.29), channel_id=1, source_target_pairs={{0,96},{16,112},{32,128},{48,144},{64,160},{80,176},{96,192},{112,... | collective-permute-start | bytes 196616 | tf_op jit(solution)/shard_map/ppermute | solution.py:34
  16.8 0.0 collective-permute-done
  16.8 4.9 %collective-permute-start.7 = (bf16[2,64,256]{2,1,0:T(8,128)(2,1)S(1)}, bf16[2,64,256]{2,1,0:T(8,128)(2,1)S(1)}, u32[]{:S(2)}, u32[]{:S(2)}) collective-permute-start(bf16[2,64,256]{2,1,0:T(8,128)(2,1)S(1)} %get-tuple-element.27), channel_id=1, source_target_pairs={{0,128},{16,144},{32,160},{48,176},{64,192},{80,208},{96,224},{112... | collective-permute-start | bytes 196616 | tf_op jit(solution)/shard_map/ppermute | solution.py:34
  21.8 13.4 %collective-permute-done.9 = bf16[2,64,256]{2,1,0:T(8,128)(2,1)S(1)} collective-permute-done((bf16[2,64,256]{2,1,0:T(8,128)(2,1)S(1)}, bf16[2,64,256]{2,1,0:T(8,128)(2,1)S(1)}, u32[]{:S(2)}, u32[]{:S(2)}) %collective-permute-start.9) | collective-permute-done | bytes 65568 | tf_op jit(solution)/shard_map/ppermute | solution.py:34
  35.2 0.0 collective-permute-start.4
  35.2 0.0 collective-permute-done.8
  35.2 2.0 %collective-permute-start.5 = (bf16[2,256,256]{2,1,0:T(8,128)(2,1)S(1)}, bf16[2,256,256]{2,1,0:T(8,128)(2,1)S(1)}, u32[]{:S(2)}, u32[]{:S(2)}) collective-permute-start(bf16[2,256,256]{2,1,0:T(8,128)(2,1)S(1)} %get-tuple-element.21), channel_id=1, source_target_pairs={{0,224},{16,240},{32,0},{48,16},{64,32},{80,48},{96,64},{112,80},{... | collective-permute-start | bytes 786440 | tf_op jit(solution)/shard_map/ppermute | solution.py:34
  37.3 0.0 collective-permute-done.7
  37.3 3.3 %collective-permute-start.10 = (bf16[3,2,64,256]{3,2,1,0:T(8,128)(2,1)S(1)}, bf16[3,2,64,256]{3,2,1,0:T(8,128)(2,1)S(1)}, u32[]{:S(2)}, u32[]{:S(2)}) collective-permute-start(bf16[3,2,64,256]{3,2,1,0:T(8,128)(2,1)S(1)} %pad_maximum_fusion.2.own_ref), channel_id=1, source_target_pairs={{0,8},{4,12},{8,0},{12,4},{1,9},{5,13},{9,1},{13,5},{2,10},{6,14},... | collective-permute-start | bytes 589832 | tf_op jit(solution)/shard_map/ppermute | solution.py:13
  40.6 0.0 collective-permute-done.2.refs_0_
  40.6 0.7 collective-permute-start.11
  41.3 0.0 collective-permute-done.3.refs_1_
  41.3 2.6 %collective-permute-start.12 = (bf16[3,2,64,256]{3,2,1,0:T(8,128)(2,1)S(1)}, bf16[3,2,64,256]{3,2,1,0:T(8,128)(2,1)S(1)}, u32[]{:S(2)}, u32[]{:S(2)}) collective-permute-start(bf16[3,2,64,256]{3,2,1,0:T(8,128)(2,1)S(1)} %pad_maximum_fusion.2.own_ref), channel_id=1, source_target_pairs={{0,12},{4,0},{8,4},{12,8},{1,13},{5,1},{9,5},{13,9},{2,14},{6,2},{... | collective-permute-start | bytes 589832 | tf_op jit(solution)/shard_map/ppermute | solution.py:13
  43.8 0.0 collective-permute-done.4.refs_2_
  43.9 0.0 collective-permute-done.5.refs_3_
  43.9 1.5 %shard_map.67.sum_ref = f32[1024,256]{1,0:T(8,128)S(1)} custom-call(bf16[1024,4096]{1,0:T(8,128)(2,1)S(1)} %bitcast.42, bf16[256,256]{1,0:T(8,128)(2,1)S(1)} %slice_bitcast_fusion.1.kept_ref, bf16[256,256]{1,0:T(8,128)(2,1)S(1)} %slice_bitcast_fusion.came_ref, bf16[2,256,256]{2,1,0:T(8,128)(2,1)S(1)} %collective-permute-done.2.refs_0_, ...), custom_call_target="tpu_custom_call" | custom-call | flops 1342177280 | bytes 6553600 | tf_op jit(solution)/shard_map/pallas_call | solution.py:205
  45.4 0.0 collective-permute-done.10.across_ref
  45.4 2.3 %collective-permute-done.11.before_ref = bf16[3,2,64,256]{3,2,1,0:T(8,128)(2,1)S(1)} collective-permute-done((bf16[3,2,64,256]{3,2,1,0:T(8,128)(2,1)S(1)}, bf16[3,2,64,256]{3,2,1,0:T(8,128)(2,1)S(1)}, u32[]{:S(2)}, u32[]{:S(2)}) %collective-permute-start.11) | collective-permute-done | bytes 196640 | tf_op jit(solution)/shard_map/ppermute | solution.py:13
  47.7 0.0 collective-permute-done.12.after_ref
  47.7 0.6 shard_map.68
  48.3 0.0 copy-start.2
  48.4 1.6 %collective-permute-start.13 = (bf16[512,256]{1,0:T(8,128)(2,1)S(1)}, bf16[512,256]{1,0:T(8,128)(2,1)S(1)}, u32[]{:S(2)}, u32[]{:S(2)}) collective-permute-start(bf16[512,256]{1,0:T(8,128)(2,1)S(1)} %shard_map.68), channel_id=1, source_target_pairs={{0,1},{1,0},{2,3},{3,2},{4,5},{5,4},{6,7},{7,6},{8,9},{9,8},{10,11... | collective-permute-start | bytes 786440 | tf_op jit(solution)/shard_map/ppermute | solution.py:18
  49.9 0.6 shard_map.69
  50.5 2.2 %collective-permute-start.15 = (bf16[512,256]{1,0:T(8,128)(2,1)S(1)}, bf16[512,256]{1,0:T(8,128)(2,1)S(1)}, u32[]{:S(2)}, u32[]{:S(2)}) collective-permute-start(bf16[512,256]{1,0:T(8,128)(2,1)S(1)} %shard_map.69), channel_id=1, source_target_pairs={{0,3},{1,2},{2,1},{3,0},{4,7},{5,6},{6,5},{7,4},{8,11},{9,10},{10,... | collective-permute-start | bytes 786440 | tf_op jit(solution)/shard_map/ppermute | solution.py:23
  52.7 2.2 %collective-permute-done.13 = bf16[512,256]{1,0:T(8,128)(2,1)S(1)} collective-permute-done((bf16[512,256]{1,0:T(8,128)(2,1)S(1)}, bf16[512,256]{1,0:T(8,128)(2,1)S(1)}, u32[]{:S(2)}, u32[]{:S(2)}) %collective-permute-start.13) | collective-permute-done | bytes 262176 | tf_op jit(solution)/shard_map/ppermute | solution.py:18
  54.9 0.1 add_convert_fusion.1
  55.0 2.8 %collective-permute-start.14 = (bf16[512,256]{1,0:T(8,128)(2,1)S(1)}, bf16[512,256]{1,0:T(8,128)(2,1)S(1)}, u32[]{:S(2)}, u32[]{:S(2)}) collective-permute-start(bf16[512,256]{1,0:T(8,128)(2,1)S(1)} %add_convert_fusion.1), channel_id=1, source_target_pairs={{0,3},{1,2},{2,1},{3,0},{4,7},{5,6},{6,5},{7,4},{8,11},{9,10},{10,... | collective-permute-start | bytes 786440 | tf_op jit(solution)/shard_map/ppermute | solution.py:23
  57.8 2.3 %collective-permute-done.15 = bf16[512,256]{1,0:T(8,128)(2,1)S(1)} collective-permute-done((bf16[512,256]{1,0:T(8,128)(2,1)S(1)}, bf16[512,256]{1,0:T(8,128)(2,1)S(1)}, u32[]{:S(2)}, u32[]{:S(2)}) %collective-permute-start.15) | collective-permute-done | bytes 262176 | tf_op jit(solution)/shard_map/ppermute | solution.py:23
  60.2 0.1 add_convert_fusion
  60.2 0.1 collective-permute-start.16
  60.3 3.5 %collective-permute-done.14 = bf16[512,256]{1,0:T(8,128)(2,1)S(1)} collective-permute-done((bf16[512,256]{1,0:T(8,128)(2,1)S(1)}, bf16[512,256]{1,0:T(8,128)(2,1)S(1)}, u32[]{:S(2)}, u32[]{:S(2)}) %collective-permute-start.14) | collective-permute-done | bytes 262176 | tf_op jit(solution)/shard_map/ppermute | solution.py:23
  63.8 2.9 %collective-permute-done.16 = bf16[512,256]{1,0:T(8,128)(2,1)S(1)} collective-permute-done((bf16[512,256]{1,0:T(8,128)(2,1)S(1)}, bf16[512,256]{1,0:T(8,128)(2,1)S(1)}, u32[]{:S(2)}, u32[]{:S(2)}) %collective-permute-start.16) | collective-permute-done | bytes 262176 | tf_op jit(solution)/shard_map/ppermute | solution.py:18
  66.7 0.2 fusion.9
  66.9 0.7 fusion.2
  67.6 12.9 %all_to_all.5 = bf16[4,64,1024]{2,1,0:T(8,128)(2,1)S(1)} all-to-all(bf16[4,64,1024]{2,1,0:T(8,128)(2,1)S(1)} %bitcast.48), channel_id=1, replica_groups=mesh['front'=16,'row'=4,'col'=4] {'row'}, dimensions={0} | all-to-all | bytes 1048576 | tf_op jit(solution)/shard_map/all_to_all | solution.py:269
  80.5 0.8 convert_reduce_fusion
  (10 shorter events, 0.2 us)
Async XLA Ops:
  0.0 66.9 %copy-start = (bf16[1,1024,1024]{2,1,0:T(8,128)(2,1)S(1)}, bf16[1,1024,1024]{2,1,0:T(8,128)(2,1)}, u32[]{:S(2)}) copy-start(bf16[1,1024,1024]{2,1,0:T(8,128)(2,1)} %param.11) | copy-start | bytes 6291460
  3.4 2.7 %collective-permute-start.1 = (bf16[2,256,256]{2,1,0:T(8,128)(2,1)S(1)}, bf16[2,256,256]{2,1,0:T(8,128)(2,1)S(1)}, u32[]{:S(2)}, u32[]{:S(2)}) collective-permute-start(bf16[2,256,256]{2,1,0:T(8,128)(2,1)S(1)} %get-tuple-element.18), channel_id=1, source_target_pairs={{0,16},{16,0},{32,48},{48,32},{64,80},{80,64},{96,112},{112,96},{1... | collective-permute-start | bytes 786440 | tf_op jit(solution)/shard_map/ppermute | solution.py:18
  3.5 40.4 %copy-start.1 = (bf16[1,1024,4096]{2,1,0:T(8,128)(2,1)S(1)}, bf16[1,1024,4096]{2,1,0:T(8,128)(2,1)}, u32[]{:S(2)}) copy-start(bf16[1,1024,4096]{2,1,0:T(8,128)(2,1)} %param.9) | copy-start | bytes 25165828
  5.3 11.5 %collective-permute-start = (bf16[3,256,256]{2,1,0:T(8,128)(2,1)S(1)}, bf16[3,256,256]{2,1,0:T(8,128)(2,1)S(1)}, u32[]{:S(2)}, u32[]{:S(2)}) collective-permute-start(bf16[3,256,256]{2,1,0:T(8,128)(2,1)S(1)} %get-tuple-element.16), channel_id=1, source_target_pairs={{0,16},{16,0},{32,48},{48,32},{64,80},{80,64},{96,112},{112,96},{1... | collective-permute-start | bytes 1179656 | tf_op jit(solution)/shard_map/ppermute | solution.py:18
  5.9 5.8 %collective-permute-start.6 = (bf16[3,64,256]{2,1,0:T(8,128)(2,1)S(1)}, bf16[3,64,256]{2,1,0:T(8,128)(2,1)S(1)}, u32[]{:S(2)}, u32[]{:S(2)}) collective-permute-start(bf16[3,64,256]{2,1,0:T(8,128)(2,1)S(1)} %get-tuple-element.20), channel_id=1, source_target_pairs={{0,16},{16,0},{32,48},{48,32},{64,80},{80,64},{96,112},{112,96},{1... | collective-permute-start | bytes 294920 | tf_op jit(solution)/shard_map/ppermute | solution.py:18
  6.1 34.5 %collective-permute-start.2 = (bf16[2,256,256]{2,1,0:T(8,128)(2,1)S(1)}, bf16[2,256,256]{2,1,0:T(8,128)(2,1)S(1)}, u32[]{:S(2)}, u32[]{:S(2)}) collective-permute-start(bf16[2,256,256]{2,1,0:T(8,128)(2,1)S(1)} %get-tuple-element.26), channel_id=1, source_target_pairs={{0,64},{16,80},{32,96},{48,112},{64,128},{80,144},{96,160},{112,17... | collective-permute-start | bytes 786440 | tf_op jit(solution)/shard_map/ppermute | solution.py:34
  9.4 31.8 %collective-permute-start.3 = (bf16[2,256,256]{2,1,0:T(8,128)(2,1)S(1)}, bf16[2,256,256]{2,1,0:T(8,128)(2,1)S(1)}, u32[]{:S(2)}, u32[]{:S(2)}) collective-permute-start(bf16[2,256,256]{2,1,0:T(8,128)(2,1)S(1)} %get-tuple-element.25), channel_id=1, source_target_pairs={{0,192},{16,208},{32,224},{48,240},{64,0},{80,16},{96,32},{112,48}... | collective-permute-start | bytes 786440 | tf_op jit(solution)/shard_map/ppermute | solution.py:34
  11.7 23.5 %collective-permute-start.9 = (bf16[2,64,256]{2,1,0:T(8,128)(2,1)S(1)}, bf16[2,64,256]{2,1,0:T(8,128)(2,1)S(1)}, u32[]{:S(2)}, u32[]{:S(2)}) collective-permute-start(bf16[2,64,256]{2,1,0:T(8,128)(2,1)S(1)} %get-tuple-element.28), channel_id=1, source_target_pairs={{0,160},{16,176},{32,192},{48,208},{64,224},{80,240},{96,0},{112,1... | collective-permute-start | bytes 196616 | tf_op jit(solution)/shard_map/ppermute | solution.py:34
  15.1 20.2 %collective-permute-start.8 = (bf16[2,64,256]{2,1,0:T(8,128)(2,1)S(1)}, bf16[2,64,256]{2,1,0:T(8,128)(2,1)S(1)}, u32[]{:S(2)}, u32[]{:S(2)}) collective-permute-start(bf16[2,64,256]{2,1,0:T(8,128)(2,1)S(1)} %get-tuple-element.29), channel_id=1, source_target_pairs={{0,96},{16,112},{32,128},{48,144},{64,160},{80,176},{96,192},{112,... | collective-permute-start | bytes 196616 | tf_op jit(solution)/shard_map/ppermute | solution.py:34
  16.8 20.4 %collective-permute-start.7 = (bf16[2,64,256]{2,1,0:T(8,128)(2,1)S(1)}, bf16[2,64,256]{2,1,0:T(8,128)(2,1)S(1)}, u32[]{:S(2)}, u32[]{:S(2)}) collective-permute-start(bf16[2,64,256]{2,1,0:T(8,128)(2,1)S(1)} %get-tuple-element.27), channel_id=1, source_target_pairs={{0,128},{16,144},{32,160},{48,176},{64,192},{80,208},{96,224},{112... | collective-permute-start | bytes 196616 | tf_op jit(solution)/shard_map/ppermute | solution.py:34
  35.2 8.6 %collective-permute-start.4 = (bf16[2,256,256]{2,1,0:T(8,128)(2,1)S(1)}, bf16[2,256,256]{2,1,0:T(8,128)(2,1)S(1)}, u32[]{:S(2)}, u32[]{:S(2)}) collective-permute-start(bf16[2,256,256]{2,1,0:T(8,128)(2,1)S(1)} %get-tuple-element.22), channel_id=1, source_target_pairs={{0,32},{16,48},{32,64},{48,80},{64,96},{80,112},{96,128},{112,144}... | collective-permute-start | bytes 786440 | tf_op jit(solution)/shard_map/ppermute | solution.py:34
  35.2 8.6 %collective-permute-start.5 = (bf16[2,256,256]{2,1,0:T(8,128)(2,1)S(1)}, bf16[2,256,256]{2,1,0:T(8,128)(2,1)S(1)}, u32[]{:S(2)}, u32[]{:S(2)}) collective-permute-start(bf16[2,256,256]{2,1,0:T(8,128)(2,1)S(1)} %get-tuple-element.21), channel_id=1, source_target_pairs={{0,224},{16,240},{32,0},{48,16},{64,32},{80,48},{96,64},{112,80},{... | collective-permute-start | bytes 786440 | tf_op jit(solution)/shard_map/ppermute | solution.py:34
  37.3 8.1 %collective-permute-start.10 = (bf16[3,2,64,256]{3,2,1,0:T(8,128)(2,1)S(1)}, bf16[3,2,64,256]{3,2,1,0:T(8,128)(2,1)S(1)}, u32[]{:S(2)}, u32[]{:S(2)}) collective-permute-start(bf16[3,2,64,256]{3,2,1,0:T(8,128)(2,1)S(1)} %pad_maximum_fusion.2.own_ref), channel_id=1, source_target_pairs={{0,8},{4,12},{8,0},{12,4},{1,9},{5,13},{9,1},{13,5},{2,10},{6,14},... | collective-permute-start | bytes 589832 | tf_op jit(solution)/shard_map/ppermute | solution.py:13
  40.6 7.1 %collective-permute-start.11 = (bf16[3,2,64,256]{3,2,1,0:T(8,128)(2,1)S(1)}, bf16[3,2,64,256]{3,2,1,0:T(8,128)(2,1)S(1)}, u32[]{:S(2)}, u32[]{:S(2)}) collective-permute-start(bf16[3,2,64,256]{3,2,1,0:T(8,128)(2,1)S(1)} %pad_maximum_fusion.2.own_ref), channel_id=1, source_target_pairs={{0,4},{4,8},{8,12},{12,0},{1,5},{5,9},{9,13},{13,1},{2,6},{6,10},{... | collective-permute-start | bytes 589832 | tf_op jit(solution)/shard_map/ppermute | solution.py:13
  41.3 6.4 %collective-permute-start.12 = (bf16[3,2,64,256]{3,2,1,0:T(8,128)(2,1)S(1)}, bf16[3,2,64,256]{3,2,1,0:T(8,128)(2,1)S(1)}, u32[]{:S(2)}, u32[]{:S(2)}) collective-permute-start(bf16[3,2,64,256]{3,2,1,0:T(8,128)(2,1)S(1)} %pad_maximum_fusion.2.own_ref), channel_id=1, source_target_pairs={{0,12},{4,0},{8,4},{12,8},{1,13},{5,1},{9,5},{13,9},{2,14},{6,2},{... | collective-permute-start | bytes 589832 | tf_op jit(solution)/shard_map/ppermute | solution.py:13
  48.3 18.3 %copy-start.2 = (bf16[1,1024,256]{2,1,0:T(8,128)(2,1)S(1)}, bf16[1,1024,256]{2,1,0:T(8,128)(2,1)}, u32[]{:S(2)}) copy-start(bf16[1,1024,256]{2,1,0:T(8,128)(2,1)} %param.10) | copy-start | bytes 1572868
  48.4 6.6 %collective-permute-start.13 = (bf16[512,256]{1,0:T(8,128)(2,1)S(1)}, bf16[512,256]{1,0:T(8,128)(2,1)S(1)}, u32[]{:S(2)}, u32[]{:S(2)}) collective-permute-start(bf16[512,256]{1,0:T(8,128)(2,1)S(1)} %shard_map.68), channel_id=1, source_target_pairs={{0,1},{1,0},{2,3},{3,2},{4,5},{5,4},{6,7},{7,6},{8,9},{9,8},{10,11... | collective-permute-start | bytes 786440 | tf_op jit(solution)/shard_map/ppermute | solution.py:18
  50.5 9.6 %collective-permute-start.15 = (bf16[512,256]{1,0:T(8,128)(2,1)S(1)}, bf16[512,256]{1,0:T(8,128)(2,1)S(1)}, u32[]{:S(2)}, u32[]{:S(2)}) collective-permute-start(bf16[512,256]{1,0:T(8,128)(2,1)S(1)} %shard_map.69), channel_id=1, source_target_pairs={{0,3},{1,2},{2,1},{3,0},{4,7},{5,6},{6,5},{7,4},{8,11},{9,10},{10,... | collective-permute-start | bytes 786440 | tf_op jit(solution)/shard_map/ppermute | solution.py:23
  55.0 8.9 %collective-permute-start.14 = (bf16[512,256]{1,0:T(8,128)(2,1)S(1)}, bf16[512,256]{1,0:T(8,128)(2,1)S(1)}, u32[]{:S(2)}, u32[]{:S(2)}) collective-permute-start(bf16[512,256]{1,0:T(8,128)(2,1)S(1)} %add_convert_fusion.1), channel_id=1, source_target_pairs={{0,3},{1,2},{2,1},{3,0},{4,7},{5,6},{6,5},{7,4},{8,11},{9,10},{10,... | collective-permute-start | bytes 786440 | tf_op jit(solution)/shard_map/ppermute | solution.py:23
  60.2 6.5 %collective-permute-start.16 = (bf16[512,256]{1,0:T(8,128)(2,1)S(1)}, bf16[512,256]{1,0:T(8,128)(2,1)S(1)}, u32[]{:S(2)}, u32[]{:S(2)}) collective-permute-start(bf16[512,256]{1,0:T(8,128)(2,1)S(1)} %add_convert_fusion), channel_id=1, source_target_pairs={{0,1},{1,0},{2,3},{3,2},{4,5},{5,4},{6,7},{7,6},{8,9},{9,8},{10,11... | collective-permute-start | bytes 786440 | tf_op jit(solution)/shard_map/ppermute | solution.py:18
where the time goes:
time: 81.4 us; the launch traced here: 81.3 us
  starting transfers between devices  31.6 us (39%)
  waiting for transfers between devices  26.6 us (33%)
  blocking collectives  12.9 us (16%)
  Pallas kernels  7.99 us (10%)
  other arithmetic  1.24 us (2%)
    ppermute x7, starting transfers between devices, along_chips(): lax.ppermute(shard, 'front', [(i, (i + 2 * step) % peers) for i in range(...  17.6 us
    ppermute x7, waiting for transfers between devices, along_chips(): lax.ppermute(shard, 'front', [(i, (i + 2 * step) % peers) for i in range(...  13.5 us
    all_to_all x1, blocking collectives, per_device(): tiles = lax.all_to_all(tiles, 'row', 0, 0, tiled=True)  12.9 us
    ppermute x3, starting transfers between devices, shifted(): lax.ppermute(shard, axis, [(i, (i + step) % peers) for i in range(peers)])  6.52 us
    ppermute x2, waiting for transfers between devices, odd_swap(): lax.ppermute(shard, axis, [(i, (i + (1 if i % 2 else -1)) % peers) for i...  5.86 us
    ppermute x5, waiting for transfers between devices, even_swap(): return lax.ppermute(shard, axis, [(i, i ^ 1) for i in range(peers)])  5.04 us
    ppermute x2, starting transfers between devices, odd_swap(): lax.ppermute(shard, axis, [(i, (i + (1 if i % 2 else -1)) % peers) for i...  5.02 us
    pallas_call x2, Pallas kernels, pick_slots(): pl.pallas_call(functools.partial(pick_slots_kernel, steps), out_shape=(sh...  3.16 us
  transfers between devices with their start and end apart: 17, of which 6 were waited for; matrix products, arithmetic and copies ran while one was open for 0% of the time, Pallas kernels for 5%

commit v1 on v0

--- a/solution.py
+++ b/solution.py
@@ -23,15 +23,20 @@
     return lax.ppermute(shard, axis, [(i, (i + (1 if i % 2 else -1)) % peers) for i in range(peers)])
 
 
-FAR = (4, 3, -3)
-MID = (2, -2)
-NEAR = (1, -1, 0)
+FAR = ((4, 4), (3, 3), (-3, -3), (-2, 2))
+MID = ((2, -2),)
+NEAR = ((1, 1), (-1, -1), (0, 0))
 CHIPS = 8
 
 
 def along_chips(shard, step):
     peers = lax.axis_size("front")
-    return lax.ppermute(shard, "front", [(i, (i + 2 * step) % peers) for i in range(peers)])
+    return lax.ppermute(shard, "front", [(i, (i + 2 * step[i % 2]) % peers) for i in range(peers)])
+
+
+def moved(chip, step, core, sign):
+    here = step[0] + core * (step[1] - step[0])
+    return lax.rem(chip + sign * here + CHIPS, CHIPS)
 
 
 def place():
@@ -75,8 +80,8 @@
 
     chosen = []
     for step in FAR:
-        target = 2 * lax.rem(chip + step + CHIPS, CHIPS)
-        kept, sent = rolled(target + core, 0), rolled(target + 1 - core, share)
+        kept = rolled(2 * moved(chip, step, core, 1) + core, 0)
+        sent = rolled(2 * moved(chip, step, 1 - core, 1) + 1 - core, share)
         chosen.append(jnp.where(lane < share, kept, sent))
     copies[2].wait()
     for i, index in enumerate(chosen):
@@ -89,9 +94,8 @@
     chip, core = place()
     ancestor = held_ref[...]
     for i, step in enumerate(steps):
-        target = 2 * lax.rem(chip + step + CHIPS, CHIPS)
-        for d, ref in ((target + 1 - core, sent_ref), (target + core, kept_ref)):
-            ref[i] = picked_rows(ancestor, live_ref[d])
+        for to, ref in ((1 - core, sent_ref), (core, kept_ref)):
+            ref[i] = picked_rows(ancestor, live_ref[2 * moved(chip, step, to, 1) + to])
 
 
 def pick_shares(counts, lists, ancestor):
@@ -156,7 +160,7 @@
                 lax.bitwise_xor(core, holder)
             ]
         sum_ref[...] += jnp.dot(
-            columns(coeff_ref, lax.rem(chip - step + CHIPS, CHIPS), 0, pivots),
+            columns(coeff_ref, moved(chip, step, core, -1), 0, pivots),
             rows_ref[i],
             preferred_element_type=jnp.float32,
         )
@@ -183,7 +187,7 @@
                 start = (holder * peers + block) * share
                 rows_ref[i, start : start + share, :] = piece
         total = total + jnp.dot(
-            columns(coeff_ref, lax.rem(chip - step + CHIPS, CHIPS), part * half, half),
+            columns(coeff_ref, moved(chip, step, core, -1), part * half, half),
             rows_ref[i],
             preferred_element_type=jnp.float32,
         )
@@ -205,11 +209,11 @@
     total = pl.pallas_call(
         near_kernel,
         out_shape=jax.ShapeDtypeStruct((pivots, sources), jnp.float32),
-        in_specs=[vmem] * 7,
+        in_specs=[vmem] * (len(MID + NEAR) + 2),
         out_specs=vmem,
         scratch_shapes=[pltpu.VMEM((len(MID + NEAR), depth, sources), coeff.dtype)],
         compiler_params=pltpu.CompilerParams(vmem_limit_bytes=24 << 20),
-        cost_estimate=cost(5),
+        cost_estimate=cost(len(MID + NEAR)),
     )(coeff, kept, came, *mid, *near)
     half = jax.ShapeDtypeStruct((pivots // 2, sources), coeff.dtype)
     return [
@@ -244,8 +248,8 @@
     for part, steps in ((near, NEAR[:2]), (far, FAR), (mid, MID)):
         for i, step in enumerate(steps):
             sent.append(along_chips(part[i], step))
-    near_parts, shares, mid_parts = sent[:2], jnp.stack(sent[2:5]), sent[5:]
-    shares = [shares]
+    near_parts, mid_parts = sent[:2], sent[2 + len(FAR) :]
+    shares = [jnp.stack(sent[2 : 2 + len(FAR)])]
     for step in (2, 1, -1):
         shares.append(shifted(shares[0], "row", step))
     coeff = pltpu.with_memory_space_constraint(border_coeff[0], pltpu.VMEM)

time: 81.4 us -> 77.8 us (0.956)
  the two profiles are of different devices: /device:TPU:32 before, /device:TPU:64 now
where the time goes in v1:
time: 77.8 us; the launch traced here: 77.7 us
  starting transfers between devices  31.3 us (40%)
  waiting for transfers between devices  24.3 us (31%)
  blocking collectives  12.3 us (16%)
  Pallas kernels  7.61 us (10%)
  other arithmetic  1.24 us (2%)
    ppermute x7, starting transfers between devices, along_chips(): lax.ppermute(shard, 'front', [(i, (i + 2 * step[i % 2]) % peers) for i in...  17.2 us
    all_to_all x1, blocking collectives, per_device(): tiles = lax.all_to_all(tiles, 'row', 0, 0, tiled=True)  12.3 us
    ppermute x3, waiting for transfers between devices, shifted(): lax.ppermute(shard, axis, [(i, (i + step) % peers) for i in range(peers)])  8 us
    ppermute x3, starting transfers between devices, shifted(): lax.ppermute(shard, axis, [(i, (i + step) % peers) for i in range(peers)])  6.57 us
    ppermute x5, waiting for transfers between devices, even_swap(): return lax.ppermute(shard, axis, [(i, i ^ 1) for i in range(peers)])  5.77 us
    ppermute x2, waiting for transfers between devices, odd_swap(): lax.ppermute(shard, axis, [(i, (i + (1 if i % 2 else -1)) % peers) for i...  5.69 us
    ppermute x2, starting transfers between devices, odd_swap(): lax.ppermute(shard, axis, [(i, (i + (1 if i % 2 else -1)) % peers) for i...  5.16 us
    ppermute x7, waiting for transfers between devices, along_chips(): lax.ppermute(shard, 'front', [(i, (i + 2 * step[i % 2]) % peers) for i in...  4.81 us
  transfers between devices with their start and end apart: 17, of which 11 were waited for; matrix products, arithmetic and copies ran while one was open for 0% of the time, Pallas kernels for 4%

profile of v1, /device:TPU:64, one launch (start us, length us, event | category | flops | bytes accessed | tf_op | source)
XLA Modules:
  0.0 77.7 jit_solution(3851226740677939483)
XLA Ops:
  0.0 2.2 %shard_map.64 = (bf16[4,64,256]{2,1,0:T(8,128)(2,1)S(1)}, bf16[4,64,256]{2,1,0:T(8,128)(2,1)S(1)}, s32[16,1,256]{2,1,0:T(1,128)S(1)}, bf16[2048,256]{1,0:T(8,128)(2,1)S(1)}) custom-call(s32[16]{0:T(128)} %bitcast.57, s32[1,16,1,256]{3,2,1,0:T(1,128)} %lists_hbm.1, bf16[2048,256]{1,0:T(8,128)(2,1)} %ancestor_hbm.1), custom_call_target="tpu_custom_call" | custom-call | tf_op jit(solution)/shard_map/pallas_call | solution.py:105
  2.2 0.0 copy-start.1
  2.2 1.9 %shard_map.65 = (bf16[3,256,256]{2,1,0:T(8,128)(2,1)S(1)}, bf16[3,256,256]{2,1,0:T(8,128)(2,1)S(1)}) custom-call(s32[16,1,256]{2,1,0:T(1,128)S(1)} %get-tuple-element.13.live_ref, bf16[2048,256]{1,0:T(8,128)(2,1)S(1)} %get-tuple-element.14.held_ref), custom_call_target="tpu_custom_call" | custom-call | flops 1610612736 | bytes 1048576 | tf_op jit(solution)/shard_map/pallas_call | solution.py:127
  4.1 0.1 collective-permute-start
  4.2 0.8 %shard_map.66 = (bf16[1,256,256]{2,1,0:T(8,128)(2,1)S(1)}, bf16[1,256,256]{2,1,0:T(8,128)(2,1)S(1)}) custom-call(s32[16,1,256]{2,1,0:T(1,128)S(1)} %get-tuple-element.13.live_ref, bf16[2048,256]{1,0:T(8,128)(2,1)S(1)} %get-tuple-element.14.held_ref), custom_call_target="tpu_custom_call" | custom-call | flops 536870912 | bytes 1048576 | tf_op jit(solution)/shard_map/pallas_call | solution.py:127
  5.0 0.6 collective-permute-start.1
  5.6 0.1 collective-permute-start.5
  5.7 0.9 %collective-permute-done.1 = bf16[1,256,256]{2,1,0:T(8,128)(2,1)S(1)} collective-permute-done((bf16[1,256,256]{2,1,0:T(8,128)(2,1)S(1)}, bf16[1,256,256]{2,1,0:T(8,128)(2,1)S(1)}, u32[]{:S(2)}, u32[]{:S(2)}) %collective-permute-start.1) | collective-permute-done | bytes 131104 | tf_op jit(solution)/shard_map/ppermute | solution.py:18
  6.6 4.6 %collective-permute-start.2 = (bf16[2,256,256]{2,1,0:T(8,128)(2,1)S(1)}, bf16[2,256,256]{2,1,0:T(8,128)(2,1)S(1)}, u32[]{:S(2)}, u32[]{:S(2)}) collective-permute-start(bf16[2,256,256]{2,1,0:T(8,128)(2,1)S(1)} %maximum_bitcast_fusion.1), channel_id=1, source_target_pairs={{0,64},{16,208},{32,96},{48,240},{64,128},{80,16},{96,160},{112,48... | collective-permute-start | bytes 786440 | tf_op jit(solution)/shard_map/ppermute | solution.py:34
  11.1 0.0 collective-permute-done.5
  11.2 0.1 collective-permute-start.9
  11.3 3.4 %collective-permute-start.8 = (bf16[2,64,256]{2,1,0:T(8,128)(2,1)S(1)}, bf16[2,64,256]{2,1,0:T(8,128)(2,1)S(1)}, u32[]{:S(2)}, u32[]{:S(2)}) collective-permute-start(bf16[2,64,256]{2,1,0:T(8,128)(2,1)S(1)} %get-tuple-element.28), channel_id=1, source_target_pairs={{0,160},{16,176},{32,192},{48,208},{64,224},{80,240},{96,0},{112,1... | collective-permute-start | bytes 196616 | tf_op jit(solution)/shard_map/ppermute | solution.py:34
  14.6 1.7 %collective-permute-start.7 = (bf16[2,64,256]{2,1,0:T(8,128)(2,1)S(1)}, bf16[2,64,256]{2,1,0:T(8,128)(2,1)S(1)}, u32[]{:S(2)}, u32[]{:S(2)}) collective-permute-start(bf16[2,64,256]{2,1,0:T(8,128)(2,1)S(1)} %get-tuple-element.26), channel_id=1, source_target_pairs={{0,96},{16,112},{32,128},{48,144},{64,160},{80,176},{96,192},{112,... | collective-permute-start | bytes 196616 | tf_op jit(solution)/shard_map/ppermute | solution.py:34
  16.4 0.0 collective-permute-done
  16.4 3.7 %collective-permute-start.6 = (bf16[2,64,256]{2,1,0:T(8,128)(2,1)S(1)}, bf16[2,64,256]{2,1,0:T(8,128)(2,1)S(1)}, u32[]{:S(2)}, u32[]{:S(2)}) collective-permute-start(bf16[2,64,256]{2,1,0:T(8,128)(2,1)S(1)} %get-tuple-element.25), channel_id=1, source_target_pairs={{0,128},{16,144},{32,160},{48,176},{64,192},{80,208},{96,224},{112... | collective-permute-start | bytes 196616 | tf_op jit(solution)/shard_map/ppermute | solution.py:34
  20.2 0.0 collective-permute-done.9
  20.2 2.0 %collective-permute-start.3 = (bf16[2,256,256]{2,1,0:T(8,128)(2,1)S(1)}, bf16[2,256,256]{2,1,0:T(8,128)(2,1)S(1)}, u32[]{:S(2)}, u32[]{:S(2)}) collective-permute-start(bf16[2,256,256]{2,1,0:T(8,128)(2,1)S(1)} %get-tuple-element.22), channel_id=1, source_target_pairs={{0,32},{16,48},{32,64},{48,80},{64,96},{80,112},{96,128},{112,144}... | collective-permute-start | bytes 786440 | tf_op jit(solution)/shard_map/ppermute | solution.py:34
  22.2 0.7 collective-permute-done.8
  22.9 1.6 %collective-permute-start.4 = (bf16[2,256,256]{2,1,0:T(8,128)(2,1)S(1)}, bf16[2,256,256]{2,1,0:T(8,128)(2,1)S(1)}, u32[]{:S(2)}, u32[]{:S(2)}) collective-permute-start(bf16[2,256,256]{2,1,0:T(8,128)(2,1)S(1)} %get-tuple-element.21), channel_id=1, source_target_pairs={{0,224},{16,240},{32,0},{48,16},{64,32},{80,48},{96,64},{112,80},{... | collective-permute-start | bytes 786440 | tf_op jit(solution)/shard_map/ppermute | solution.py:34
  24.5 1.2 %collective-permute-done.7 = bf16[2,64,256]{2,1,0:T(8,128)(2,1)S(1)} collective-permute-done((bf16[2,64,256]{2,1,0:T(8,128)(2,1)S(1)}, bf16[2,64,256]{2,1,0:T(8,128)(2,1)S(1)}, u32[]{:S(2)}, u32[]{:S(2)}) %collective-permute-start.7) | collective-permute-done | bytes 65568 | tf_op jit(solution)/shard_map/ppermute | solution.py:34
  25.7 3.0 %collective-permute-done.6 = bf16[2,64,256]{2,1,0:T(8,128)(2,1)S(1)} collective-permute-done((bf16[2,64,256]{2,1,0:T(8,128)(2,1)S(1)}, bf16[2,64,256]{2,1,0:T(8,128)(2,1)S(1)}, u32[]{:S(2)}, u32[]{:S(2)}) %collective-permute-start.6) | collective-permute-done | bytes 65568 | tf_op jit(solution)/shard_map/ppermute | solution.py:34
  28.7 3.3 %collective-permute-start.10 = (bf16[4,2,64,256]{3,2,1,0:T(8,128)(2,1)S(1)}, bf16[4,2,64,256]{3,2,1,0:T(8,128)(2,1)S(1)}, u32[]{:S(2)}, u32[]{:S(2)}) collective-permute-start(bf16[4,2,64,256]{3,2,1,0:T(8,128)(2,1)S(1)} %pad_maximum_fusion.1.own_ref), channel_id=1, source_target_pairs={{0,8},{4,12},{8,0},{12,4},{1,9},{5,13},{9,1},{13,5},{2,10},{6,14},... | collective-permute-start | bytes 786440 | tf_op jit(solution)/shard_map/ppermute | solution.py:13
  32.0 0.7 collective-permute-start.11
  32.7 0.0 collective-permute-done.2.refs_0_
  32.7 2.6 %collective-permute-start.12 = (bf16[4,2,64,256]{3,2,1,0:T(8,128)(2,1)S(1)}, bf16[4,2,64,256]{3,2,1,0:T(8,128)(2,1)S(1)}, u32[]{:S(2)}, u32[]{:S(2)}) collective-permute-start(bf16[4,2,64,256]{3,2,1,0:T(8,128)(2,1)S(1)} %pad_maximum_fusion.1.own_ref), channel_id=1, source_target_pairs={{0,12},{4,0},{8,4},{12,8},{1,13},{5,1},{9,5},{13,9},{2,14},{6,2},{... | collective-permute-start | bytes 786440 | tf_op jit(solution)/shard_map/ppermute | solution.py:13
  35.3 0.0 collective-permute-done.3.refs_1_
  35.3 0.0 collective-permute-done.4.refs_2_
  35.3 1.3 %shard_map.67.sum_ref = f32[1024,256]{1,0:T(8,128)S(1)} custom-call(bf16[1024,4096]{1,0:T(8,128)(2,1)S(1)} %bitcast.43, bf16[256,256]{1,0:T(8,128)(2,1)S(1)} %slice_bitcast_fusion.1.kept_ref, bf16[256,256]{1,0:T(8,128)(2,1)S(1)} %slice_bitcast_fusion.came_ref, bf16[2,256,256]{2,1,0:T(8,128)(2,1)S(1)} %collective-permute-done.2.refs_0_, ...), custom_call_target="tpu_custom_call" | custom-call | flops 1073741824 | bytes 5242880 | tf_op jit(solution)/shard_map/pallas_call | solution.py:209
  36.6 2.9 %collective-permute-done.10.across_ref = bf16[4,2,64,256]{3,2,1,0:T(8,128)(2,1)S(1)} collective-permute-done((bf16[4,2,64,256]{3,2,1,0:T(8,128)(2,1)S(1)}, bf16[4,2,64,256]{3,2,1,0:T(8,128)(2,1)S(1)}, u32[]{:S(2)}, u32[]{:S(2)}) %collective-permute-start.10) | collective-permute-done | bytes 262176 | tf_op jit(solution)/shard_map/ppermute | solution.py:13
  39.5 4.7 %collective-permute-done.11.before_ref = bf16[4,2,64,256]{3,2,1,0:T(8,128)(2,1)S(1)} collective-permute-done((bf16[4,2,64,256]{3,2,1,0:T(8,128)(2,1)S(1)}, bf16[4,2,64,256]{3,2,1,0:T(8,128)(2,1)S(1)}, u32[]{:S(2)}, u32[]{:S(2)}) %collective-permute-start.11) | collective-permute-done | bytes 262176 | tf_op jit(solution)/shard_map/ppermute | solution.py:13
  44.2 0.4 collective-permute-done.12.after_ref
  44.6 0.8 shard_map.68
  45.4 0.0 copy-start.2
  45.4 1.5 %collective-permute-start.13 = (bf16[512,256]{1,0:T(8,128)(2,1)S(1)}, bf16[512,256]{1,0:T(8,128)(2,1)S(1)}, u32[]{:S(2)}, u32[]{:S(2)}) collective-permute-start(bf16[512,256]{1,0:T(8,128)(2,1)S(1)} %shard_map.68), channel_id=1, source_target_pairs={{0,1},{1,0},{2,3},{3,2},{4,5},{5,4},{6,7},{7,6},{8,9},{9,8},{10,11... | collective-permute-start | bytes 786440 | tf_op jit(solution)/shard_map/ppermute | solution.py:18
  46.9 0.8 shard_map.69
  47.7 2.2 %collective-permute-start.15 = (bf16[512,256]{1,0:T(8,128)(2,1)S(1)}, bf16[512,256]{1,0:T(8,128)(2,1)S(1)}, u32[]{:S(2)}, u32[]{:S(2)}) collective-permute-start(bf16[512,256]{1,0:T(8,128)(2,1)S(1)} %shard_map.69), channel_id=1, source_target_pairs={{0,3},{1,2},{2,1},{3,0},{4,7},{5,6},{6,5},{7,4},{8,11},{9,10},{10,... | collective-permute-start | bytes 786440 | tf_op jit(solution)/shard_map/ppermute | solution.py:23
  49.9 3.4 %collective-permute-done.13 = bf16[512,256]{1,0:T(8,128)(2,1)S(1)} collective-permute-done((bf16[512,256]{1,0:T(8,128)(2,1)S(1)}, bf16[512,256]{1,0:T(8,128)(2,1)S(1)}, u32[]{:S(2)}, u32[]{:S(2)}) %collective-permute-start.13) | collective-permute-done | bytes 262176 | tf_op jit(solution)/shard_map/ppermute | solution.py:18
  53.3 0.1 add_convert_fusion.1
  53.3 3.0 %collective-permute-start.14 = (bf16[512,256]{1,0:T(8,128)(2,1)S(1)}, bf16[512,256]{1,0:T(8,128)(2,1)S(1)}, u32[]{:S(2)}, u32[]{:S(2)}) collective-permute-start(bf16[512,256]{1,0:T(8,128)(2,1)S(1)} %add_convert_fusion.1), channel_id=1, source_target_pairs={{0,3},{1,2},{2,1},{3,0},{4,7},{5,6},{6,5},{7,4},{8,11},{9,10},{10,... | collective-permute-start | bytes 786440 | tf_op jit(solution)/shard_map/ppermute | solution.py:23
  56.3 0.8 %collective-permute-done.15 = bf16[512,256]{1,0:T(8,128)(2,1)S(1)} collective-permute-done((bf16[512,256]{1,0:T(8,128)(2,1)S(1)}, bf16[512,256]{1,0:T(8,128)(2,1)S(1)}, u32[]{:S(2)}, u32[]{:S(2)}) %collective-permute-start.15) | collective-permute-done | bytes 262176 | tf_op jit(solution)/shard_map/ppermute | solution.py:23
  57.1 0.1 add_convert_fusion
  57.2 0.1 collective-permute-start.16
  57.3 4.9 %collective-permute-done.14 = bf16[512,256]{1,0:T(8,128)(2,1)S(1)} collective-permute-done((bf16[512,256]{1,0:T(8,128)(2,1)S(1)}, bf16[512,256]{1,0:T(8,128)(2,1)S(1)}, u32[]{:S(2)}, u32[]{:S(2)}) %collective-permute-start.14) | collective-permute-done | bytes 262176 | tf_op jit(solution)/shard_map/ppermute | solution.py:23
  62.2 1.5 %collective-permute-done.16 = bf16[512,256]{1,0:T(8,128)(2,1)S(1)} collective-permute-done((bf16[512,256]{1,0:T(8,128)(2,1)S(1)}, bf16[512,256]{1,0:T(8,128)(2,1)S(1)}, u32[]{:S(2)}, u32[]{:S(2)}) %collective-permute-start.16) | collective-permute-done | bytes 262176 | tf_op jit(solution)/shard_map/ppermute | solution.py:18
  63.7 0.2 fusion.9
  63.9 0.7 fusion.2
  64.6 12.3 %all_to_all.5 = bf16[4,64,1024]{2,1,0:T(8,128)(2,1)S(1)} all-to-all(bf16[4,64,1024]{2,1,0:T(8,128)(2,1)S(1)} %bitcast.49), channel_id=1, replica_groups=mesh['front'=16,'row'=4,'col'=4] {'row'}, dimensions={0} | all-to-all | bytes 1048576 | tf_op jit(solution)/shard_map/all_to_all | solution.py:273
  76.9 0.8 %convert_reduce_fusion = f32[64,1024]{1,0:T(8,128)} fusion(bf16[4,64,1024]{2,1,0:T(8,128)(2,1)S(1)} %all_to_all.5), kind=kLoop, calls=%fused_computation.3 | loop fusion | flops 458752 | bytes 786432 | tf_op jit(solution)/shard_map/reduce_sum | solution.py:274
  (10 shorter events, 0.2 us)
Async XLA Ops:
  0.0 63.9 %copy-start = (bf16[1,1024,1024]{2,1,0:T(8,128)(2,1)S(1)}, bf16[1,1024,1024]{2,1,0:T(8,128)(2,1)}, u32[]{:S(2)}) copy-start(bf16[1,1024,1024]{2,1,0:T(8,128)(2,1)} %param.11) | copy-start | bytes 6291460
  2.2 33.1 %copy-start.1 = (bf16[1,1024,4096]{2,1,0:T(8,128)(2,1)S(1)}, bf16[1,1024,4096]{2,1,0:T(8,128)(2,1)}, u32[]{:S(2)}) copy-start(bf16[1,1024,4096]{2,1,0:T(8,128)(2,1)} %param.9) | copy-start | bytes 25165828
  4.1 12.3 %collective-permute-start = (bf16[3,256,256]{2,1,0:T(8,128)(2,1)S(1)}, bf16[3,256,256]{2,1,0:T(8,128)(2,1)S(1)}, u32[]{:S(2)}, u32[]{:S(2)}) collective-permute-start(bf16[3,256,256]{2,1,0:T(8,128)(2,1)S(1)} %get-tuple-element.16), channel_id=1, source_target_pairs={{0,16},{16,0},{32,48},{48,32},{64,80},{80,64},{96,112},{112,96},{1... | collective-permute-start | bytes 1179656 | tf_op jit(solution)/shard_map/ppermute | solution.py:18
  5.0 1.6 %collective-permute-start.1 = (bf16[1,256,256]{2,1,0:T(8,128)(2,1)S(1)}, bf16[1,256,256]{2,1,0:T(8,128)(2,1)S(1)}, u32[]{:S(2)}, u32[]{:S(2)}) collective-permute-start(bf16[1,256,256]{2,1,0:T(8,128)(2,1)S(1)} %get-tuple-element.18), channel_id=1, source_target_pairs={{0,16},{16,0},{32,48},{48,32},{64,80},{80,64},{96,112},{112,96},{1... | collective-permute-start | bytes 393224 | tf_op jit(solution)/shard_map/ppermute | solution.py:18
  5.6 5.6 %collective-permute-start.5 = (bf16[4,64,256]{2,1,0:T(8,128)(2,1)S(1)}, bf16[4,64,256]{2,1,0:T(8,128)(2,1)S(1)}, u32[]{:S(2)}, u32[]{:S(2)}) collective-permute-start(bf16[4,64,256]{2,1,0:T(8,128)(2,1)S(1)} %get-tuple-element.20), channel_id=1, source_target_pairs={{0,16},{16,0},{32,48},{48,32},{64,80},{80,64},{96,112},{112,96},{1... | collective-permute-start | bytes 393224 | tf_op jit(solution)/shard_map/ppermute | solution.py:18
  6.6 26.1 %collective-permute-start.2 = (bf16[2,256,256]{2,1,0:T(8,128)(2,1)S(1)}, bf16[2,256,256]{2,1,0:T(8,128)(2,1)S(1)}, u32[]{:S(2)}, u32[]{:S(2)}) collective-permute-start(bf16[2,256,256]{2,1,0:T(8,128)(2,1)S(1)} %maximum_bitcast_fusion.1), channel_id=1, source_target_pairs={{0,64},{16,208},{32,96},{48,240},{64,128},{80,16},{96,160},{112,48... | collective-permute-start | bytes 786440 | tf_op jit(solution)/shard_map/ppermute | solution.py:34
  11.2 9.0 %collective-permute-start.9 = (bf16[2,64,256]{2,1,0:T(8,128)(2,1)S(1)}, bf16[2,64,256]{2,1,0:T(8,128)(2,1)S(1)}, u32[]{:S(2)}, u32[]{:S(2)}) collective-permute-start(bf16[2,64,256]{2,1,0:T(8,128)(2,1)S(1)} %get-tuple-element.27), channel_id=1, source_target_pairs={{0,192},{16,80},{32,224},{48,112},{64,0},{80,144},{96,32},{112,176... | collective-permute-start | bytes 196616 | tf_op jit(solution)/shard_map/ppermute | solution.py:34
  11.3 11.6 %collective-permute-start.8 = (bf16[2,64,256]{2,1,0:T(8,128)(2,1)S(1)}, bf16[2,64,256]{2,1,0:T(8,128)(2,1)S(1)}, u32[]{:S(2)}, u32[]{:S(2)}) collective-permute-start(bf16[2,64,256]{2,1,0:T(8,128)(2,1)S(1)} %get-tuple-element.28), channel_id=1, source_target_pairs={{0,160},{16,176},{32,192},{48,208},{64,224},{80,240},{96,0},{112,1... | collective-permute-start | bytes 196616 | tf_op jit(solution)/shard_map/ppermute | solution.py:34
  14.6 11.1 %collective-permute-start.7 = (bf16[2,64,256]{2,1,0:T(8,128)(2,1)S(1)}, bf16[2,64,256]{2,1,0:T(8,128)(2,1)S(1)}, u32[]{:S(2)}, u32[]{:S(2)}) collective-permute-start(bf16[2,64,256]{2,1,0:T(8,128)(2,1)S(1)} %get-tuple-element.26), channel_id=1, source_target_pairs={{0,96},{16,112},{32,128},{48,144},{64,160},{80,176},{96,192},{112,... | collective-permute-start | bytes 196616 | tf_op jit(solution)/shard_map/ppermute | solution.py:34
  16.4 12.3 %collective-permute-start.6 = (bf16[2,64,256]{2,1,0:T(8,128)(2,1)S(1)}, bf16[2,64,256]{2,1,0:T(8,128)(2,1)S(1)}, u32[]{:S(2)}, u32[]{:S(2)}) collective-permute-start(bf16[2,64,256]{2,1,0:T(8,128)(2,1)S(1)} %get-tuple-element.25), channel_id=1, source_target_pairs={{0,128},{16,144},{32,160},{48,176},{64,192},{80,208},{96,224},{112... | collective-permute-start | bytes 196616 | tf_op jit(solution)/shard_map/ppermute | solution.py:34
  20.2 15.1 %collective-permute-start.3 = (bf16[2,256,256]{2,1,0:T(8,128)(2,1)S(1)}, bf16[2,256,256]{2,1,0:T(8,128)(2,1)S(1)}, u32[]{:S(2)}, u32[]{:S(2)}) collective-permute-start(bf16[2,256,256]{2,1,0:T(8,128)(2,1)S(1)} %get-tuple-element.22), channel_id=1, source_target_pairs={{0,32},{16,48},{32,64},{48,80},{64,96},{80,112},{96,128},{112,144}... | collective-permute-start | bytes 786440 | tf_op jit(solution)/shard_map/ppermute | solution.py:34
  22.9 12.4 %collective-permute-start.4 = (bf16[2,256,256]{2,1,0:T(8,128)(2,1)S(1)}, bf16[2,256,256]{2,1,0:T(8,128)(2,1)S(1)}, u32[]{:S(2)}, u32[]{:S(2)}) collective-permute-start(bf16[2,256,256]{2,1,0:T(8,128)(2,1)S(1)} %get-tuple-element.21), channel_id=1, source_target_pairs={{0,224},{16,240},{32,0},{48,16},{64,32},{80,48},{96,64},{112,80},{... | collective-permute-start | bytes 786440 | tf_op jit(solution)/shard_map/ppermute | solution.py:34
  28.7 10.8 %collective-permute-start.10 = (bf16[4,2,64,256]{3,2,1,0:T(8,128)(2,1)S(1)}, bf16[4,2,64,256]{3,2,1,0:T(8,128)(2,1)S(1)}, u32[]{:S(2)}, u32[]{:S(2)}) collective-permute-start(bf16[4,2,64,256]{3,2,1,0:T(8,128)(2,1)S(1)} %pad_maximum_fusion.1.own_ref), channel_id=1, source_target_pairs={{0,8},{4,12},{8,0},{12,4},{1,9},{5,13},{9,1},{13,5},{2,10},{6,14},... | collective-permute-start | bytes 786440 | tf_op jit(solution)/shard_map/ppermute | solution.py:13
  32.0 12.1 %collective-permute-start.11 = (bf16[4,2,64,256]{3,2,1,0:T(8,128)(2,1)S(1)}, bf16[4,2,64,256]{3,2,1,0:T(8,128)(2,1)S(1)}, u32[]{:S(2)}, u32[]{:S(2)}) collective-permute-start(bf16[4,2,64,256]{3,2,1,0:T(8,128)(2,1)S(1)} %pad_maximum_fusion.1.own_ref), channel_id=1, source_target_pairs={{0,4},{4,8},{8,12},{12,0},{1,5},{5,9},{9,13},{13,1},{2,6},{6,10},{... | collective-permute-start | bytes 786440 | tf_op jit(solution)/shard_map/ppermute | solution.py:13
  32.7 11.9 %collective-permute-start.12 = (bf16[4,2,64,256]{3,2,1,0:T(8,128)(2,1)S(1)}, bf16[4,2,64,256]{3,2,1,0:T(8,128)(2,1)S(1)}, u32[]{:S(2)}, u32[]{:S(2)}) collective-permute-start(bf16[4,2,64,256]{3,2,1,0:T(8,128)(2,1)S(1)} %pad_maximum_fusion.1.own_ref), channel_id=1, source_target_pairs={{0,12},{4,0},{8,4},{12,8},{1,13},{5,1},{9,5},{13,9},{2,14},{6,2},{... | collective-permute-start | bytes 786440 | tf_op jit(solution)/shard_map/ppermute | solution.py:13
  45.4 18.3 %copy-start.2 = (bf16[1,1024,256]{2,1,0:T(8,128)(2,1)S(1)}, bf16[1,1024,256]{2,1,0:T(8,128)(2,1)}, u32[]{:S(2)}) copy-start(bf16[1,1024,256]{2,1,0:T(8,128)(2,1)} %param.10) | copy-start | bytes 1572868
  45.4 7.9 %collective-permute-start.13 = (bf16[512,256]{1,0:T(8,128)(2,1)S(1)}, bf16[512,256]{1,0:T(8,128)(2,1)S(1)}, u32[]{:S(2)}, u32[]{:S(2)}) collective-permute-start(bf16[512,256]{1,0:T(8,128)(2,1)S(1)} %shard_map.68), channel_id=1, source_target_pairs={{0,1},{1,0},{2,3},{3,2},{4,5},{5,4},{6,7},{7,6},{8,9},{9,8},{10,11... | collective-permute-start | bytes 786440 | tf_op jit(solution)/shard_map/ppermute | solution.py:18
  47.7 9.4 %collective-permute-start.15 = (bf16[512,256]{1,0:T(8,128)(2,1)S(1)}, bf16[512,256]{1,0:T(8,128)(2,1)S(1)}, u32[]{:S(2)}, u32[]{:S(2)}) collective-permute-start(bf16[512,256]{1,0:T(8,128)(2,1)S(1)} %shard_map.69), channel_id=1, source_target_pairs={{0,3},{1,2},{2,1},{3,0},{4,7},{5,6},{6,5},{7,4},{8,11},{9,10},{10,... | collective-permute-start | bytes 786440 | tf_op jit(solution)/shard_map/ppermute | solution.py:23
  53.3 8.8 %collective-permute-start.14 = (bf16[512,256]{1,0:T(8,128)(2,1)S(1)}, bf16[512,256]{1,0:T(8,128)(2,1)S(1)}, u32[]{:S(2)}, u32[]{:S(2)}) collective-permute-start(bf16[512,256]{1,0:T(8,128)(2,1)S(1)} %add_convert_fusion.1), channel_id=1, source_target_pairs={{0,3},{1,2},{2,1},{3,0},{4,7},{5,6},{6,5},{7,4},{8,11},{9,10},{10,... | collective-permute-start | bytes 786440 | tf_op jit(solution)/shard_map/ppermute | solution.py:23
  57.2 6.5 %collective-permute-start.16 = (bf16[512,256]{1,0:T(8,128)(2,1)S(1)}, bf16[512,256]{1,0:T(8,128)(2,1)S(1)}, u32[]{:S(2)}, u32[]{:S(2)}) collective-permute-start(bf16[512,256]{1,0:T(8,128)(2,1)S(1)} %add_convert_fusion), channel_id=1, source_target_pairs={{0,1},{1,0},{2,3},{3,2},{4,5},{5,4},{6,7},{7,6},{8,9},{9,8},{10,11... | collective-permute-start | bytes 786440 | tf_op jit(solution)/shard_map/ppermute | solution.py:18

commit v2 on v1

--- a/solution.py
+++ b/solution.py
@@ -270,8 +270,15 @@
     ).astype(jnp.bfloat16)
     peers = lax.axis_size("row")
     tiles = term.reshape(peers, term.shape[0] // peers, term.shape[1])
-    tiles = lax.all_to_all(tiles, "row", 0, 0, tiled=True)
-    return jnp.sum(tiles.astype(jnp.float32), axis=0)[None]
+    me = lax.axis_index("row")
+
+    def tile(step):
+        return lax.dynamic_index_in_dim(tiles, lax.rem(me + step, peers), 0, keepdims=False)
+
+    answer = tile(0).astype(jnp.float32)
+    for step in (2, 1, 3):
+        answer = answer + shifted(tile(step), "row", step).astype(jnp.float32)
+    return answer[None]
 
 
 def solution(mesh):

time: 77.8 us -> 77.4 us (level)
  blocking collectives: 12.3 us -> 0 us
  waiting for transfers between devices: 24.3 us -> 30.4 us
  starting transfers between devices: 31.3 us -> 36.1 us
  other arithmetic: 1.24 us -> 2.18 us
    all_to_all x1 -> x0, blocking collectives: 12.3 us -> none  [per_device(): tiles = lax.all_to_all(tiles, 'row', 0, 0, tiled=True)]
    ppermute x3 -> x6, waiting for transfers between devices: 8 us -> 14 us  [shifted(): lax.ppermute(shard, axis, [(i, (i + step) % peers) for i in range(peers)])]
    ppermute x3 -> x6, starting transfers between devices: 6.57 us -> 11.3 us  [shifted(): lax.ppermute(shard, axis, [(i, (i + step) % peers) for i in range(peers)])]
    convert_element_type x1, other arithmetic: 0.2 us -> 1.15 us  [per_device(): parts.append((rhs[rows].astype(jnp.float32) - total).astype(jnp.bfloat16))]
    reduce_sum x1 -> x0, other arithmetic: 0.78 us -> none  [per_device(): return jnp.sum(tiles.astype(jnp.float32), axis=0)[None]]
  transfers between devices with their start and end apart: 17 -> 20, of which waited for: 11 -> 13; matrix products, arithmetic and copies ran while one was open for 0% -> 0% of each run, Pallas kernels for 4% -> 4%
where the time goes in v2:
time: 77.4 us; the launch traced here: 77.3 us
  starting transfers between devices  36.1 us (47%)
  waiting for transfers between devices  30.4 us (39%)
  Pallas kernels  7.61 us (10%)
  other arithmetic  2.18 us (3%)
    ppermute x7, starting transfers between devices, along_chips(): lax.ppermute(shard, 'front', [(i, (i + 2 * step[i % 2]) % peers) for i in...  17.2 us
    ppermute x6, waiting for transfers between devices, shifted(): lax.ppermute(shard, axis, [(i, (i + step) % peers) for i in range(peers)])  14 us
    ppermute x6, starting transfers between devices, shifted(): lax.ppermute(shard, axis, [(i, (i + step) % peers) for i in range(peers)])  11.3 us
    ppermute x5, waiting for transfers between devices, even_swap(): return lax.ppermute(shard, axis, [(i, i ^ 1) for i in range(peers)])  5.87 us
    ppermute x2, waiting for transfers between devices, odd_swap(): lax.ppermute(shard, axis, [(i, (i + (1 if i % 2 else -1)) % peers) for i...  5.66 us
    ppermute x2, starting transfers between devices, odd_swap(): lax.ppermute(shard, axis, [(i, (i + (1 if i % 2 else -1)) % peers) for i...  5.16 us
    ppermute x7, waiting for transfers between devices, along_chips(): lax.ppermute(shard, 'front', [(i, (i + 2 * step[i % 2]) % peers) for i in...  4.81 us
    pallas_call x2, Pallas kernels, pick_slots(): pl.pallas_call(functools.partial(pick_slots_kernel, steps), out_shape=(sh...  2.65 us
  transfers between devices with their start and end apart: 20, of which 13 were waited for; matrix products, arithmetic and copies ran while one was open for 0% of the time, Pallas kernels for 4%

profile of v2, /device:TPU:64, one launch (start us, length us, event | category | flops | bytes accessed | tf_op | source)
XLA Modules:
  0.0 77.3 jit_solution(16315200100081818230)
XLA Ops:
  0.0 2.2 %shard_map.64 = (bf16[4,64,256]{2,1,0:T(8,128)(2,1)S(1)}, bf16[4,64,256]{2,1,0:T(8,128)(2,1)S(1)}, s32[16,1,256]{2,1,0:T(1,128)S(1)}, bf16[2048,256]{1,0:T(8,128)(2,1)S(1)}) custom-call(s32[16]{0:T(128)} %bitcast.68, s32[1,16,1,256]{3,2,1,0:T(1,128)} %lists_hbm.1, bf16[2048,256]{1,0:T(8,128)(2,1)} %ancestor_hbm.1), custom_call_target="tpu_custom_call" | custom-call | tf_op jit(solution)/shard_map/pallas_call | solution.py:105
  2.2 0.0 copy-start.1
  2.2 1.9 %shard_map.65 = (bf16[3,256,256]{2,1,0:T(8,128)(2,1)S(1)}, bf16[3,256,256]{2,1,0:T(8,128)(2,1)S(1)}) custom-call(s32[16,1,256]{2,1,0:T(1,128)S(1)} %get-tuple-element.13.live_ref, bf16[2048,256]{1,0:T(8,128)(2,1)S(1)} %get-tuple-element.14.held_ref), custom_call_target="tpu_custom_call" | custom-call | flops 1610612736 | bytes 1048576 | tf_op jit(solution)/shard_map/pallas_call | solution.py:127
  4.1 0.1 collective-permute-start
  4.2 0.8 %shard_map.66 = (bf16[1,256,256]{2,1,0:T(8,128)(2,1)S(1)}, bf16[1,256,256]{2,1,0:T(8,128)(2,1)S(1)}) custom-call(s32[16,1,256]{2,1,0:T(1,128)S(1)} %get-tuple-element.13.live_ref, bf16[2048,256]{1,0:T(8,128)(2,1)S(1)} %get-tuple-element.14.held_ref), custom_call_target="tpu_custom_call" | custom-call | flops 536870912 | bytes 1048576 | tf_op jit(solution)/shard_map/pallas_call | solution.py:127
  5.0 0.6 collective-permute-start.1
  5.6 0.1 collective-permute-start.5
  5.7 0.9 %collective-permute-done.1 = bf16[1,256,256]{2,1,0:T(8,128)(2,1)S(1)} collective-permute-done((bf16[1,256,256]{2,1,0:T(8,128)(2,1)S(1)}, bf16[1,256,256]{2,1,0:T(8,128)(2,1)S(1)}, u32[]{:S(2)}, u32[]{:S(2)}) %collective-permute-start.1) | collective-permute-done | bytes 131104 | tf_op jit(solution)/shard_map/ppermute | solution.py:18
  6.6 4.6 %collective-permute-start.2 = (bf16[2,256,256]{2,1,0:T(8,128)(2,1)S(1)}, bf16[2,256,256]{2,1,0:T(8,128)(2,1)S(1)}, u32[]{:S(2)}, u32[]{:S(2)}) collective-permute-start(bf16[2,256,256]{2,1,0:T(8,128)(2,1)S(1)} %maximum_bitcast_fusion.1), channel_id=1, source_target_pairs={{0,64},{16,208},{32,96},{48,240},{64,128},{80,16},{96,160},{112,48... | collective-permute-start | bytes 786440 | tf_op jit(solution)/shard_map/ppermute | solution.py:34
  11.1 0.0 collective-permute-done.5
  11.2 0.1 collective-permute-start.9
  11.3 3.4 %collective-permute-start.8 = (bf16[2,64,256]{2,1,0:T(8,128)(2,1)S(1)}, bf16[2,64,256]{2,1,0:T(8,128)(2,1)S(1)}, u32[]{:S(2)}, u32[]{:S(2)}) collective-permute-start(bf16[2,64,256]{2,1,0:T(8,128)(2,1)S(1)} %get-tuple-element.31), channel_id=1, source_target_pairs={{0,160},{16,176},{32,192},{48,208},{64,224},{80,240},{96,0},{112,1... | collective-permute-start | bytes 196616 | tf_op jit(solution)/shard_map/ppermute | solution.py:34
  14.6 1.7 %collective-permute-start.7 = (bf16[2,64,256]{2,1,0:T(8,128)(2,1)S(1)}, bf16[2,64,256]{2,1,0:T(8,128)(2,1)S(1)}, u32[]{:S(2)}, u32[]{:S(2)}) collective-permute-start(bf16[2,64,256]{2,1,0:T(8,128)(2,1)S(1)} %get-tuple-element.29), channel_id=1, source_target_pairs={{0,96},{16,112},{32,128},{48,144},{64,160},{80,176},{96,192},{112,... | collective-permute-start | bytes 196616 | tf_op jit(solution)/shard_map/ppermute | solution.py:34
  16.4 3.7 %collective-permute-start.6 = (bf16[2,64,256]{2,1,0:T(8,128)(2,1)S(1)}, bf16[2,64,256]{2,1,0:T(8,128)(2,1)S(1)}, u32[]{:S(2)}, u32[]{:S(2)}) collective-permute-start(bf16[2,64,256]{2,1,0:T(8,128)(2,1)S(1)} %get-tuple-element.28), channel_id=1, source_target_pairs={{0,128},{16,144},{32,160},{48,176},{64,192},{80,208},{96,224},{112... | collective-permute-start | bytes 196616 | tf_op jit(solution)/shard_map/ppermute | solution.py:34
  20.2 0.0 collective-permute-done.9
  20.2 2.0 %collective-permute-start.3 = (bf16[2,256,256]{2,1,0:T(8,128)(2,1)S(1)}, bf16[2,256,256]{2,1,0:T(8,128)(2,1)S(1)}, u32[]{:S(2)}, u32[]{:S(2)}) collective-permute-start(bf16[2,256,256]{2,1,0:T(8,128)(2,1)S(1)} %get-tuple-element.22), channel_id=1, source_target_pairs={{0,32},{16,48},{32,64},{48,80},{64,96},{80,112},{96,128},{112,144}... | collective-permute-start | bytes 786440 | tf_op jit(solution)/shard_map/ppermute | solution.py:34
  22.2 0.7 collective-permute-done.8
  22.9 1.6 %collective-permute-start.4 = (bf16[2,256,256]{2,1,0:T(8,128)(2,1)S(1)}, bf16[2,256,256]{2,1,0:T(8,128)(2,1)S(1)}, u32[]{:S(2)}, u32[]{:S(2)}) collective-permute-start(bf16[2,256,256]{2,1,0:T(8,128)(2,1)S(1)} %get-tuple-element.21), channel_id=1, source_target_pairs={{0,224},{16,240},{32,0},{48,16},{64,32},{80,48},{96,64},{112,80},{... | collective-permute-start | bytes 786440 | tf_op jit(solution)/shard_map/ppermute | solution.py:34
  24.5 1.2 %collective-permute-done.7 = bf16[2,64,256]{2,1,0:T(8,128)(2,1)S(1)} collective-permute-done((bf16[2,64,256]{2,1,0:T(8,128)(2,1)S(1)}, bf16[2,64,256]{2,1,0:T(8,128)(2,1)S(1)}, u32[]{:S(2)}, u32[]{:S(2)}) %collective-permute-start.7) | collective-permute-done | bytes 65568 | tf_op jit(solution)/shard_map/ppermute | solution.py:34
  25.7 3.0 %collective-permute-done.6 = bf16[2,64,256]{2,1,0:T(8,128)(2,1)S(1)} collective-permute-done((bf16[2,64,256]{2,1,0:T(8,128)(2,1)S(1)}, bf16[2,64,256]{2,1,0:T(8,128)(2,1)S(1)}, u32[]{:S(2)}, u32[]{:S(2)}) %collective-permute-start.6) | collective-permute-done | bytes 65568 | tf_op jit(solution)/shard_map/ppermute | solution.py:34
  28.7 3.3 %collective-permute-start.10 = (bf16[4,2,64,256]{3,2,1,0:T(8,128)(2,1)S(1)}, bf16[4,2,64,256]{3,2,1,0:T(8,128)(2,1)S(1)}, u32[]{:S(2)}, u32[]{:S(2)}) collective-permute-start(bf16[4,2,64,256]{3,2,1,0:T(8,128)(2,1)S(1)} %pad_maximum_fusion.1.own_ref), channel_id=1, source_target_pairs={{0,8},{4,12},{8,0},{12,4},{1,9},{5,13},{9,1},{13,5},{2,10},{6,14},... | collective-permute-start | bytes 786440 | tf_op jit(solution)/shard_map/ppermute | solution.py:13
  32.0 0.7 collective-permute-start.11
  32.7 2.6 %collective-permute-start.12 = (bf16[4,2,64,256]{3,2,1,0:T(8,128)(2,1)S(1)}, bf16[4,2,64,256]{3,2,1,0:T(8,128)(2,1)S(1)}, u32[]{:S(2)}, u32[]{:S(2)}) collective-permute-start(bf16[4,2,64,256]{3,2,1,0:T(8,128)(2,1)S(1)} %pad_maximum_fusion.1.own_ref), channel_id=1, source_target_pairs={{0,12},{4,0},{8,4},{12,8},{1,13},{5,1},{9,5},{13,9},{2,14},{6,2},{... | collective-permute-start | bytes 786440 | tf_op jit(solution)/shard_map/ppermute | solution.py:13
  35.3 0.0 collective-permute-done.4.refs_2_
  35.3 1.3 %shard_map.67.sum_ref = f32[1024,256]{1,0:T(8,128)S(1)} custom-call(bf16[1024,4096]{1,0:T(8,128)(2,1)S(1)} %bitcast.53, bf16[256,256]{1,0:T(8,128)(2,1)S(1)} %slice_bitcast_fusion.1.kept_ref, bf16[256,256]{1,0:T(8,128)(2,1)S(1)} %slice_bitcast_fusion.came_ref, bf16[2,256,256]{2,1,0:T(8,128)(2,1)S(1)} %collective-permute-done.2.refs_0_, ...), custom_call_target="tpu_custom_call" | custom-call | flops 1073741824 | bytes 5242880 | tf_op jit(solution)/shard_map/pallas_call | solution.py:209
  36.6 2.9 %collective-permute-done.10.across_ref = bf16[4,2,64,256]{3,2,1,0:T(8,128)(2,1)S(1)} collective-permute-done((bf16[4,2,64,256]{3,2,1,0:T(8,128)(2,1)S(1)}, bf16[4,2,64,256]{3,2,1,0:T(8,128)(2,1)S(1)}, u32[]{:S(2)}, u32[]{:S(2)}) %collective-permute-start.10) | collective-permute-done | bytes 262176 | tf_op jit(solution)/shard_map/ppermute | solution.py:13
  39.5 4.7 %collective-permute-done.11.before_ref = bf16[4,2,64,256]{3,2,1,0:T(8,128)(2,1)S(1)} collective-permute-done((bf16[4,2,64,256]{3,2,1,0:T(8,128)(2,1)S(1)}, bf16[4,2,64,256]{3,2,1,0:T(8,128)(2,1)S(1)}, u32[]{:S(2)}, u32[]{:S(2)}) %collective-permute-start.11) | collective-permute-done | bytes 262176 | tf_op jit(solution)/shard_map/ppermute | solution.py:13
  44.2 0.4 collective-permute-done.12.after_ref
  44.6 0.8 shard_map.68
  45.4 0.0 copy-start.2
  45.4 1.5 %collective-permute-start.13 = (bf16[512,256]{1,0:T(8,128)(2,1)S(1)}, bf16[512,256]{1,0:T(8,128)(2,1)S(1)}, u32[]{:S(2)}, u32[]{:S(2)}) collective-permute-start(bf16[512,256]{1,0:T(8,128)(2,1)S(1)} %shard_map.68), channel_id=1, source_target_pairs={{0,1},{1,0},{2,3},{3,2},{4,5},{5,4},{6,7},{7,6},{8,9},{9,8},{10,11... | collective-permute-start | bytes 786440 | tf_op jit(solution)/shard_map/ppermute | solution.py:18
  46.9 0.8 shard_map.69
  47.7 2.2 %collective-permute-start.15 = (bf16[512,256]{1,0:T(8,128)(2,1)S(1)}, bf16[512,256]{1,0:T(8,128)(2,1)S(1)}, u32[]{:S(2)}, u32[]{:S(2)}) collective-permute-start(bf16[512,256]{1,0:T(8,128)(2,1)S(1)} %shard_map.69), channel_id=1, source_target_pairs={{0,3},{1,2},{2,1},{3,0},{4,7},{5,6},{6,5},{7,4},{8,11},{9,10},{10,... | collective-permute-start | bytes 786440 | tf_op jit(solution)/shard_map/ppermute | solution.py:23
  49.9 3.4 %collective-permute-done.13 = bf16[512,256]{1,0:T(8,128)(2,1)S(1)} collective-permute-done((bf16[512,256]{1,0:T(8,128)(2,1)S(1)}, bf16[512,256]{1,0:T(8,128)(2,1)S(1)}, u32[]{:S(2)}, u32[]{:S(2)}) %collective-permute-start.13) | collective-permute-done | bytes 262176 | tf_op jit(solution)/shard_map/ppermute | solution.py:18
  53.3 0.1 add_convert_fusion.1
  53.3 3.0 %collective-permute-start.14 = (bf16[512,256]{1,0:T(8,128)(2,1)S(1)}, bf16[512,256]{1,0:T(8,128)(2,1)S(1)}, u32[]{:S(2)}, u32[]{:S(2)}) collective-permute-start(bf16[512,256]{1,0:T(8,128)(2,1)S(1)} %add_convert_fusion.1), channel_id=1, source_target_pairs={{0,3},{1,2},{2,1},{3,0},{4,7},{5,6},{6,5},{7,4},{8,11},{9,10},{10,... | collective-permute-start | bytes 786440 | tf_op jit(solution)/shard_map/ppermute | solution.py:23
  56.3 0.8 %collective-permute-done.15 = bf16[512,256]{1,0:T(8,128)(2,1)S(1)} collective-permute-done((bf16[512,256]{1,0:T(8,128)(2,1)S(1)}, bf16[512,256]{1,0:T(8,128)(2,1)S(1)}, u32[]{:S(2)}, u32[]{:S(2)}) %collective-permute-start.15) | collective-permute-done | bytes 262176 | tf_op jit(solution)/shard_map/ppermute | solution.py:23
  57.1 0.1 add_convert_fusion
  57.2 0.1 collective-permute-start.16
  57.3 4.8 %collective-permute-done.14 = bf16[512,256]{1,0:T(8,128)(2,1)S(1)} collective-permute-done((bf16[512,256]{1,0:T(8,128)(2,1)S(1)}, bf16[512,256]{1,0:T(8,128)(2,1)S(1)}, u32[]{:S(2)}, u32[]{:S(2)}) %collective-permute-start.14) | collective-permute-done | bytes 262176 | tf_op jit(solution)/shard_map/ppermute | solution.py:23
  62.2 1.6 %collective-permute-done.16 = bf16[512,256]{1,0:T(8,128)(2,1)} collective-permute-done((bf16[512,256]{1,0:T(8,128)(2,1)S(1)}, bf16[512,256]{1,0:T(8,128)(2,1)}, u32[]{:S(2)}, u32[]{:S(2)}) %collective-permute-start.16) | collective-permute-done | bytes 262176 | tf_op jit(solution)/shard_map/ppermute | solution.py:18
  63.8 1.1 %fusion.9 = (bf16[512,256]{1,0:T(8,128)(2,1)S(1)}, bf16[512,256]{1,0:T(8,128)(2,1)S(1)}) fusion(bf16[512,256]{1,0:T(8,128)(2,1)S(1)} %collective-permute-done.14, bf16[512,256]{1,0:T(8,128)(2,1)S(1)} %add_convert_fusion.1, bf16[1,1024,256]{2,1,0:T(8,128)(2,1)S(1)} %copy-done.2, bf16[512,256]{1,0:T(8,128)(2,1)} %collective-permute-done.16, ...), kind=kLoop, calls=%fused_computation.9 | loop fusion | flops 1572864 | bytes 2097152 | tf_op jit(solution)/shard_map/convert_element_type | solution.py:266
  64.9 0.7 fusion.2
  65.7 3.2 %collective-permute-start.19 = (bf16[64,1024]{1,0:T(8,128)(2,1)S(1)}, bf16[64,1024]{1,0:T(8,128)(2,1)S(1)}, u32[]{:S(2)}, u32[]{:S(2)}) collective-permute-start(bf16[64,1024]{1,0:T(8,128)(2,1)S(1)} %get-tuple-element.24), channel_id=1, source_target_pairs={{0,12},{4,0},{8,4},{12,8},{1,13},{5,1},{9,5},{13,9},{2,14},{6,2},{... | collective-permute-start | bytes 393224 | tf_op jit(solution)/shard_map/ppermute | solution.py:13
  68.9 1.6 %collective-permute-start.17 = (bf16[64,1024]{1,0:T(8,128)(2,1)S(1)}, bf16[64,1024]{1,0:T(8,128)(2,1)S(1)}, u32[]{:S(2)}, u32[]{:S(2)}) collective-permute-start(bf16[64,1024]{1,0:T(8,128)(2,1)S(1)} %get-tuple-element.23), channel_id=1, source_target_pairs={{0,8},{4,12},{8,0},{12,4},{1,9},{5,13},{9,1},{13,5},{2,10},{6,14},... | collective-permute-start | bytes 393224 | tf_op jit(solution)/shard_map/ppermute | solution.py:13
  70.5 2.3 %collective-permute-done.19 = bf16[64,1024]{1,0:T(8,128)(2,1)S(1)} collective-permute-done((bf16[64,1024]{1,0:T(8,128)(2,1)S(1)}, bf16[64,1024]{1,0:T(8,128)(2,1)S(1)}, u32[]{:S(2)}, u32[]{:S(2)}) %collective-permute-start.19) | collective-permute-done | bytes 131104 | tf_op jit(solution)/shard_map/ppermute | solution.py:13
  72.7 3.8 %collective-permute-done.18 = bf16[64,1024]{1,0:T(8,128)(2,1)S(1)} collective-permute-done((bf16[64,1024]{1,0:T(8,128)(2,1)S(1)}, bf16[64,1024]{1,0:T(8,128)(2,1)S(1)}, u32[]{:S(2)}, u32[]{:S(2)}) %collective-permute-start.18) | collective-permute-done | bytes 131104 | tf_op jit(solution)/shard_map/ppermute | solution.py:13
  76.5 0.8 fusion.13
  (16 shorter events, 0.2 us)
Async XLA Ops:
  0.0 64.9 %copy-start = (bf16[1,1024,1024]{2,1,0:T(8,128)(2,1)S(1)}, bf16[1,1024,1024]{2,1,0:T(8,128)(2,1)}, u32[]{:S(2)}) copy-start(bf16[1,1024,1024]{2,1,0:T(8,128)(2,1)} %param.11) | copy-start | bytes 6291460
  2.2 33.1 %copy-start.1 = (bf16[1,1024,4096]{2,1,0:T(8,128)(2,1)S(1)}, bf16[1,1024,4096]{2,1,0:T(8,128)(2,1)}, u32[]{:S(2)}) copy-start(bf16[1,1024,4096]{2,1,0:T(8,128)(2,1)} %param.9) | copy-start | bytes 25165828
  4.1 12.3 %collective-permute-start = (bf16[3,256,256]{2,1,0:T(8,128)(2,1)S(1)}, bf16[3,256,256]{2,1,0:T(8,128)(2,1)S(1)}, u32[]{:S(2)}, u32[]{:S(2)}) collective-permute-start(bf16[3,256,256]{2,1,0:T(8,128)(2,1)S(1)} %get-tuple-element.16), channel_id=1, source_target_pairs={{0,16},{16,0},{32,48},{48,32},{64,80},{80,64},{96,112},{112,96},{1... | collective-permute-start | bytes 1179656 | tf_op jit(solution)/shard_map/ppermute | solution.py:18
  5.0 1.6 %collective-permute-start.1 = (bf16[1,256,256]{2,1,0:T(8,128)(2,1)S(1)}, bf16[1,256,256]{2,1,0:T(8,128)(2,1)S(1)}, u32[]{:S(2)}, u32[]{:S(2)}) collective-permute-start(bf16[1,256,256]{2,1,0:T(8,128)(2,1)S(1)} %get-tuple-element.18), channel_id=1, source_target_pairs={{0,16},{16,0},{32,48},{48,32},{64,80},{80,64},{96,112},{112,96},{1... | collective-permute-start | bytes 393224 | tf_op jit(solution)/shard_map/ppermute | solution.py:18
  5.6 5.6 %collective-permute-start.5 = (bf16[4,64,256]{2,1,0:T(8,128)(2,1)S(1)}, bf16[4,64,256]{2,1,0:T(8,128)(2,1)S(1)}, u32[]{:S(2)}, u32[]{:S(2)}) collective-permute-start(bf16[4,64,256]{2,1,0:T(8,128)(2,1)S(1)} %get-tuple-element.20), channel_id=1, source_target_pairs={{0,16},{16,0},{32,48},{48,32},{64,80},{80,64},{96,112},{112,96},{1... | collective-permute-start | bytes 393224 | tf_op jit(solution)/shard_map/ppermute | solution.py:18
  6.6 26.1 %collective-permute-start.2 = (bf16[2,256,256]{2,1,0:T(8,128)(2,1)S(1)}, bf16[2,256,256]{2,1,0:T(8,128)(2,1)S(1)}, u32[]{:S(2)}, u32[]{:S(2)}) collective-permute-start(bf16[2,256,256]{2,1,0:T(8,128)(2,1)S(1)} %maximum_bitcast_fusion.1), channel_id=1, source_target_pairs={{0,64},{16,208},{32,96},{48,240},{64,128},{80,16},{96,160},{112,48... | collective-permute-start | bytes 786440 | tf_op jit(solution)/shard_map/ppermute | solution.py:34
  11.2 9.0 %collective-permute-start.9 = (bf16[2,64,256]{2,1,0:T(8,128)(2,1)S(1)}, bf16[2,64,256]{2,1,0:T(8,128)(2,1)S(1)}, u32[]{:S(2)}, u32[]{:S(2)}) collective-permute-start(bf16[2,64,256]{2,1,0:T(8,128)(2,1)S(1)} %get-tuple-element.30), channel_id=1, source_target_pairs={{0,192},{16,80},{32,224},{48,112},{64,0},{80,144},{96,32},{112,176... | collective-permute-start | bytes 196616 | tf_op jit(solution)/shard_map/ppermute | solution.py:34
  11.3 11.6 %collective-permute-start.8 = (bf16[2,64,256]{2,1,0:T(8,128)(2,1)S(1)}, bf16[2,64,256]{2,1,0:T(8,128)(2,1)S(1)}, u32[]{:S(2)}, u32[]{:S(2)}) collective-permute-start(bf16[2,64,256]{2,1,0:T(8,128)(2,1)S(1)} %get-tuple-element.31), channel_id=1, source_target_pairs={{0,160},{16,176},{32,192},{48,208},{64,224},{80,240},{96,0},{112,1... | collective-permute-start | bytes 196616 | tf_op jit(solution)/shard_map/ppermute | solution.py:34
  14.6 11.1 %collective-permute-start.7 = (bf16[2,64,256]{2,1,0:T(8,128)(2,1)S(1)}, bf16[2,64,256]{2,1,0:T(8,128)(2,1)S(1)}, u32[]{:S(2)}, u32[]{:S(2)}) collective-permute-start(bf16[2,64,256]{2,1,0:T(8,128)(2,1)S(1)} %get-tuple-element.29), channel_id=1, source_target_pairs={{0,96},{16,112},{32,128},{48,144},{64,160},{80,176},{96,192},{112,... | collective-permute-start | bytes 196616 | tf_op jit(solution)/shard_map/ppermute | solution.py:34
  16.4 12.3 %collective-permute-start.6 = (bf16[2,64,256]{2,1,0:T(8,128)(2,1)S(1)}, bf16[2,64,256]{2,1,0:T(8,128)(2,1)S(1)}, u32[]{:S(2)}, u32[]{:S(2)}) collective-permute-start(bf16[2,64,256]{2,1,0:T(8,128)(2,1)S(1)} %get-tuple-element.28), channel_id=1, source_target_pairs={{0,128},{16,144},{32,160},{48,176},{64,192},{80,208},{96,224},{112... | collective-permute-start | bytes 196616 | tf_op jit(solution)/shard_map/ppermute | solution.py:34
  20.2 15.1 %collective-permute-start.3 = (bf16[2,256,256]{2,1,0:T(8,128)(2,1)S(1)}, bf16[2,256,256]{2,1,0:T(8,128)(2,1)S(1)}, u32[]{:S(2)}, u32[]{:S(2)}) collective-permute-start(bf16[2,256,256]{2,1,0:T(8,128)(2,1)S(1)} %get-tuple-element.22), channel_id=1, source_target_pairs={{0,32},{16,48},{32,64},{48,80},{64,96},{80,112},{96,128},{112,144}... | collective-permute-start | bytes 786440 | tf_op jit(solution)/shard_map/ppermute | solution.py:34
  22.9 12.4 %collective-permute-start.4 = (bf16[2,256,256]{2,1,0:T(8,128)(2,1)S(1)}, bf16[2,256,256]{2,1,0:T(8,128)(2,1)S(1)}, u32[]{:S(2)}, u32[]{:S(2)}) collective-permute-start(bf16[2,256,256]{2,1,0:T(8,128)(2,1)S(1)} %get-tuple-element.21), channel_id=1, source_target_pairs={{0,224},{16,240},{32,0},{48,16},{64,32},{80,48},{96,64},{112,80},{... | collective-permute-start | bytes 786440 | tf_op jit(solution)/shard_map/ppermute | solution.py:34
  28.7 10.8 %collective-permute-start.10 = (bf16[4,2,64,256]{3,2,1,0:T(8,128)(2,1)S(1)}, bf16[4,2,64,256]{3,2,1,0:T(8,128)(2,1)S(1)}, u32[]{:S(2)}, u32[]{:S(2)}) collective-permute-start(bf16[4,2,64,256]{3,2,1,0:T(8,128)(2,1)S(1)} %pad_maximum_fusion.1.own_ref), channel_id=1, source_target_pairs={{0,8},{4,12},{8,0},{12,4},{1,9},{5,13},{9,1},{13,5},{2,10},{6,14},... | collective-permute-start | bytes 786440 | tf_op jit(solution)/shard_map/ppermute | solution.py:13
  32.0 12.1 %collective-permute-start.11 = (bf16[4,2,64,256]{3,2,1,0:T(8,128)(2,1)S(1)}, bf16[4,2,64,256]{3,2,1,0:T(8,128)(2,1)S(1)}, u32[]{:S(2)}, u32[]{:S(2)}) collective-permute-start(bf16[4,2,64,256]{3,2,1,0:T(8,128)(2,1)S(1)} %pad_maximum_fusion.1.own_ref), channel_id=1, source_target_pairs={{0,4},{4,8},{8,12},{12,0},{1,5},{5,9},{9,13},{13,1},{2,6},{6,10},{... | collective-permute-start | bytes 786440 | tf_op jit(solution)/shard_map/ppermute | solution.py:13
  32.7 11.9 %collective-permute-start.12 = (bf16[4,2,64,256]{3,2,1,0:T(8,128)(2,1)S(1)}, bf16[4,2,64,256]{3,2,1,0:T(8,128)(2,1)S(1)}, u32[]{:S(2)}, u32[]{:S(2)}) collective-permute-start(bf16[4,2,64,256]{3,2,1,0:T(8,128)(2,1)S(1)} %pad_maximum_fusion.1.own_ref), channel_id=1, source_target_pairs={{0,12},{4,0},{8,4},{12,8},{1,13},{5,1},{9,5},{13,9},{2,14},{6,2},{... | collective-permute-start | bytes 786440 | tf_op jit(solution)/shard_map/ppermute | solution.py:13
  45.4 18.4 %copy-start.2 = (bf16[1,1024,256]{2,1,0:T(8,128)(2,1)S(1)}, bf16[1,1024,256]{2,1,0:T(8,128)(2,1)}, u32[]{:S(2)}) copy-start(bf16[1,1024,256]{2,1,0:T(8,128)(2,1)} %param.10) | copy-start | bytes 1572868
  45.4 7.9 %collective-permute-start.13 = (bf16[512,256]{1,0:T(8,128)(2,1)S(1)}, bf16[512,256]{1,0:T(8,128)(2,1)S(1)}, u32[]{:S(2)}, u32[]{:S(2)}) collective-permute-start(bf16[512,256]{1,0:T(8,128)(2,1)S(1)} %shard_map.68), channel_id=1, source_target_pairs={{0,1},{1,0},{2,3},{3,2},{4,5},{5,4},{6,7},{7,6},{8,9},{9,8},{10,11... | collective-permute-start | bytes 786440 | tf_op jit(solution)/shard_map/ppermute | solution.py:18
  47.7 9.4 %collective-permute-start.15 = (bf16[512,256]{1,0:T(8,128)(2,1)S(1)}, bf16[512,256]{1,0:T(8,128)(2,1)S(1)}, u32[]{:S(2)}, u32[]{:S(2)}) collective-permute-start(bf16[512,256]{1,0:T(8,128)(2,1)S(1)} %shard_map.69), channel_id=1, source_target_pairs={{0,3},{1,2},{2,1},{3,0},{4,7},{5,6},{6,5},{7,4},{8,11},{9,10},{10,... | collective-permute-start | bytes 786440 | tf_op jit(solution)/shard_map/ppermute | solution.py:23
  53.3 8.8 %collective-permute-start.14 = (bf16[512,256]{1,0:T(8,128)(2,1)S(1)}, bf16[512,256]{1,0:T(8,128)(2,1)S(1)}, u32[]{:S(2)}, u32[]{:S(2)}) collective-permute-start(bf16[512,256]{1,0:T(8,128)(2,1)S(1)} %add_convert_fusion.1), channel_id=1, source_target_pairs={{0,3},{1,2},{2,1},{3,0},{4,7},{5,6},{6,5},{7,4},{8,11},{9,10},{10,... | collective-permute-start | bytes 786440 | tf_op jit(solution)/shard_map/ppermute | solution.py:23
  57.2 6.6 %collective-permute-start.16 = (bf16[512,256]{1,0:T(8,128)(2,1)S(1)}, bf16[512,256]{1,0:T(8,128)(2,1)}, u32[]{:S(2)}, u32[]{:S(2)}) collective-permute-start(bf16[512,256]{1,0:T(8,128)(2,1)S(1)} %add_convert_fusion), channel_id=1, source_target_pairs={{0,1},{1,0},{2,3},{3,2},{4,5},{5,4},{6,7},{7,6},{8,9},{9,8},{10,11... | collective-permute-start | bytes 786440 | tf_op jit(solution)/shard_map/ppermute | solution.py:18
  65.7 7.0 %collective-permute-start.19 = (bf16[64,1024]{1,0:T(8,128)(2,1)S(1)}, bf16[64,1024]{1,0:T(8,128)(2,1)S(1)}, u32[]{:S(2)}, u32[]{:S(2)}) collective-permute-start(bf16[64,1024]{1,0:T(8,128)(2,1)S(1)} %get-tuple-element.24), channel_id=1, source_target_pairs={{0,12},{4,0},{8,4},{12,8},{1,13},{5,1},{9,5},{13,9},{2,14},{6,2},{... | collective-permute-start | bytes 393224 | tf_op jit(solution)/shard_map/ppermute | solution.py:13
  68.9 7.6 %collective-permute-start.18 = (bf16[64,1024]{1,0:T(8,128)(2,1)S(1)}, bf16[64,1024]{1,0:T(8,128)(2,1)S(1)}, u32[]{:S(2)}, u32[]{:S(2)}) collective-permute-start(bf16[64,1024]{1,0:T(8,128)(2,1)S(1)} %get-tuple-element.25), channel_id=1, source_target_pairs={{0,4},{4,8},{8,12},{12,0},{1,5},{5,9},{9,13},{13,1},{2,6},{6,10},{... | collective-permute-start | bytes 393224 | tf_op jit(solution)/shard_map/ppermute | solution.py:13
  68.9 7.6 %collective-permute-start.17 = (bf16[64,1024]{1,0:T(8,128)(2,1)S(1)}, bf16[64,1024]{1,0:T(8,128)(2,1)S(1)}, u32[]{:S(2)}, u32[]{:S(2)}) collective-permute-start(bf16[64,1024]{1,0:T(8,128)(2,1)S(1)} %get-tuple-element.23), channel_id=1, source_target_pairs={{0,8},{4,12},{8,0},{12,4},{1,9},{5,13},{9,1},{13,5},{2,10},{6,14},... | collective-permute-start | bytes 393224 | tf_op jit(solution)/shard_map/ppermute | solution.py:13
